TPU v7x, 128 devices: a whole 4x4x4 slice. The times are simulated.
128 devices in a mesh: sub: 32 (over y, z_hi, x), surf: 4 (over z_lo, core).
Axes of the slice: x: 4, y: 4, z: 4 (z_hi: 2, z_lo: 2; z = z_hi * 2 + z_lo), core: 2. Of those that a mesh axis runs over, the one named last changes fastest.
Arguments:
- heights: float32 [128, 512, 512], P('sub', 'surf'), may hold values from -21 to 21
- masks: int32 [4], replicated, may hold values from 1 to 31
- offsets: int32 [4, 128], replicated, may hold values from 128 to 383
- sections: int32 [128, 1], P('sub'), may hold values from 0 to 3; in each aligned block of 4 rows (0 to 3, 4 to 7, ...) at most 2 rows name the same one
- row_starts: int32 [128], P('sub'), may hold values from 0 to 888
- col_blocks: int32 [128], P('sub'), may hold values from 0 to 2
- surface: float32 [1024, 2048], P('sub', 'surf'), may hold values from -6 to 6
Outputs:
- params: float32 [4, 128], P(None, 'sub')
- fitted: float32 [1024, 2048], P('sub', 'surf')
Inputs may be any that keep to these rules, and one draw needn't show every extreme that they name: `sections`: every draw has one section receiving exactly 2 subapertures of some sub index; no section receives more than 2 of one sub index.
All inputs are finite; a program needn't handle non-finite values.
Results may differ from a plain program's by a relative error of at most 0.0003.
Values sent between devices are 32-bit elements; how exact they have to be, the bound alone decides.
A program may use at most 128 MiB of HBM per device.

v0:
```python
import jax
import jax.numpy as jnp
from jax import lax
from jax.sharding import PartitionSpec as P

HIGH = lax.Precision.HIGHEST


def partner(block, axis, stride):
    count = lax.axis_size(axis)
    route = []
    for low in range(count):
        high = low | 1 << stride
        if high != low and high < count:
            route += [(low, high), (high, low)]
    return lax.ppermute(block, axis, route)


def spline(t):
    t2 = t * t
    t3 = t2 * t
    first = t3 / 6.0
    second = (-3.0 * t3 + 12.0 * t2 - 12.0 * t + 4.0) / 6.0
    third = (3.0 * t3 - 24.0 * t2 + 60.0 * t - 44.0) / 6.0
    fourth = (4.0 - t) * (4.0 - t) * (4.0 - t) / 6.0
    inner = jnp.where(t < 1.0, first, jnp.where(t < 2.0, second, jnp.where(t < 3.0, third, fourth)))
    return jnp.where((t < 0.0) | (t >= 4.0), jnp.zeros_like(t), inner)


def spline_table(count_rows, count_cols):
    row_ids = jnp.arange(count_rows, dtype=jnp.int32).astype(jnp.float32)[:, None]
    col_ids = jnp.arange(count_cols, dtype=jnp.int32).astype(jnp.float32)[None, :]
    return spline(row_ids * 0.25 - col_ids + 3.0)


def per_device(heights, masks, offsets, sections, row_starts, col_blocks, surface):
    sub_dev, rows_dev, pix = heights.shape
    rounds = masks.shape[0]
    n_sub = lax.axis_size("sub")
    n_surf = lax.axis_size("surf")
    me_sub = lax.axis_index("sub")
    me_surf = lax.axis_index("surf")
    block = pix // 4
    window_rows = rows_dev // 4 + 8
    capacity = max(2, sub_dev // 2)
    sec_cols = surface.shape[1]
    coords = (jnp.arange(pix, dtype=jnp.int32).astype(jnp.float32) - (pix - 1) * 0.5) / (pix * 0.5)
    row_ids = me_surf * rows_dev + jnp.arange(rows_dev, dtype=jnp.int32)
    row_coords = (row_ids.astype(jnp.float32) - (pix - 1) * 0.5) / (pix * 0.5)
    xgrid = jnp.broadcast_to(coords[None, :], (rows_dev, pix))
    ygrid = jnp.broadcast_to(row_coords[:, None], (rows_dev, pix))
    basis = jnp.stack(
        [jnp.ones((rows_dev, pix), jnp.float32), xgrid, ygrid, xgrid * xgrid + ygrid * ygrid]
    )
    cross = jnp.einsum("kyx,lyx->klx", basis, basis, precision=HIGH)
    xidx = jnp.arange(pix, dtype=jnp.int32)
    partners = []
    for r in range(rounds):
        moving = heights
        for bit in range(n_sub.bit_length() - 1):
            swapped = partner(moving, "sub", bit)
            moving = jnp.where(masks[r] >> bit & 1 == 1, swapped, moving)
        partners.append(moving)
    partner_tiles = jnp.stack(partners)
    gram = jnp.zeros((sub_dev, 4, 4), jnp.float32)
    rhs = jnp.zeros((sub_dev, 4), jnp.float32)
    for r in range(rounds):
        partner_owner = jnp.bitwise_xor(me_sub, masks[r])
        lower = me_sub < partner_owner
        pair_start = jnp.minimum(me_sub, partner_owner) * sub_dev
        shift = lax.dynamic_slice_in_dim(offsets[r], pair_start, sub_dev)
        moved = jax.vmap(lambda tile, k: jnp.roll(tile, k, axis=1))(
            partner_tiles[r], jnp.where(lower, shift, -shift)
        )
        inside = jnp.where(
            lower, xidx[None, :] >= shift[:, None], xidx[None, :] < pix - shift[:, None]
        ).astype(jnp.float32)
        gram = gram + jnp.einsum("klx,jx->jkl", cross, inside, precision=HIGH)
        diff = (heights - moved) * inside[:, None, :]
        rhs = rhs + jnp.einsum("kyx,jyx->jk", basis, jnp.tanh(0.5 * diff), precision=HIGH)
    gram, rhs = lax.psum((gram, rhs), "surf")
    factor = jnp.linalg.cholesky(gram)
    params = jax.scipy.linalg.cho_solve((factor, True), rhs[:, :, None])[:, :, 0]
    corrected = heights - jnp.einsum("jk,kyx->jyx", params, basis, precision=HIGH)
    local = jnp.arange(sub_dev, dtype=jnp.int32)
    section_of = sections[:, 0]
    earlier = (section_of[:, None] == section_of[None, :]) & (local[None, :] < local[:, None])
    slot_of = jnp.sum(earlier.astype(jnp.int32), axis=1)
    onehot = (
        (section_of[None, None, :] == jnp.arange(n_surf, dtype=jnp.int32)[:, None, None])
        & (slot_of[None, None, :] == jnp.arange(capacity, dtype=jnp.int32)[None, :, None])
    ).astype(jnp.int32)
    onehot_float = onehot.astype(jnp.float32)
    own_slots = lax.dynamic_index_in_dim(onehot, me_surf, 0, keepdims=False)
    slot_valid = jnp.sum(own_slots, axis=1)
    slot_row = jnp.sum(own_slots * row_starts[None, :], axis=1)
    slot_col = jnp.sum(own_slots * col_blocks[None, :], axis=1) * block
    whole_section = lax.all_gather(surface, "sub", axis=0, tiled=True)
    row_table = spline_table(rows_dev, window_rows)
    col_table = spline_table(pix, 2 * block)
    weight_rows = jnp.sum(row_table * row_table, axis=0)
    weight_cols = jnp.sum(col_table * col_table, axis=0)
    diag_piece = weight_rows[:, None] * weight_cols[None, :]
    part_ids = jnp.arange(n_surf, dtype=jnp.int32)

    def cut_one(part, slot_index):
        ystart = slot_row[slot_index] + part * (rows_dev // 4)
        return lax.dynamic_slice(
            whole_section, (ystart, slot_col[slot_index]), (window_rows, 2 * block)
        )

    slot_ids = jnp.arange(capacity, dtype=jnp.int32)
    windows = jax.vmap(
        lambda part: jax.vmap(lambda slot_index: cut_one(part, slot_index))(slot_ids)
    )(part_ids)
    outgoing = jnp.einsum("tcj,jyx->tcyx", onehot_float, corrected, precision=HIGH)
    arrived = lax.all_to_all(outgoing, "surf", split_axis=0, concat_axis=0, tiled=True)
    lifted = jnp.einsum("ra,tcab->tcrb", row_table, windows, precision=HIGH)
    estimate = jnp.einsum("tcrb,pb->tcrp", lifted, col_table, precision=HIGH)
    resid = (arrived - estimate) * slot_valid.astype(jnp.float32)[None, :, None, None]
    narrowed = jnp.einsum("tcrp,pb->tcrb", resid, col_table, precision=HIGH)
    projected = jnp.einsum("ra,tcrb->tcab", row_table, narrowed, precision=HIGH)

    def add_slot(index, total):
        part = index // capacity
        slot_index = index % capacity
        ystart = slot_row[slot_index] + part * (rows_dev // 4)
        xstart = slot_col[slot_index]
        old = lax.dynamic_slice(total, (ystart, xstart), (window_rows, 2 * block))
        total = lax.dynamic_update_slice(total, old + projected[part, slot_index], (ystart, xstart))
        old_diag = lax.dynamic_slice(total, (ystart, sec_cols + xstart), (window_rows, 2 * block))
        scaled = diag_piece * slot_valid[slot_index].astype(jnp.float32)
        return lax.dynamic_update_slice(total, old_diag + scaled, (ystart, sec_cols + xstart))

    totals = jnp.zeros((whole_section.shape[0], 2 * sec_cols), jnp.float32)
    totals = lax.fori_loop(0, n_surf * capacity, add_slot, totals)
    summed = lax.psum_scatter(totals, "sub", scatter_dimension=0, tiled=True)
    fitted = surface + summed[:, :sec_cols] / (summed[:, sec_cols:] + 1.0)
    return (params.T, fitted)


def solution(mesh):
    in_specs = (
        P("sub", "surf", None),
        P(),
        P(),
        P("sub", None),
        P("sub"),
        P("sub"),
        P("sub", "surf"),
    )
    out_specs = (P(None, "sub"), P("sub", "surf"))
    return jax.shard_map(
        per_device, mesh=mesh, in_specs=in_specs, out_specs=out_specs, check_vma=False
    )
```

profile of v0, /device:TPU:0, one launch (start us, length us, event | category | flops | bytes accessed | tf_op | source)
XLA Modules:
  0.0 744.1 jit_solution(12871520380747299681)
XLA Ops:
  18.1 4.3 convolution_bitcast_fusion.1
  26.0 8.4 %collective-permute-done = f32[4,128,512]{1,0,2:T(4,128)} collective-permute-done((f32[4,128,512]{1,0,2:T(4,128)S(1)}, f32[4,128,512]{1,0,2:T(4,128)}, u32[]{:S(2)}, u32[]{:S(2)}) %collective-permute-start) | collective-permute-done | bytes 1048608 | tf_op jit(solution)/shard_map/ppermute | solution.py:16
  34.4 3.0 broadcast_select_fusion.15
  37.4 3.3 collective-permute-start.1
  44.9 3.4 collective-permute-start.9
  48.5 17.9 %collective-permute-done.1 = f32[4,128,512]{1,0,2:T(4,128)} collective-permute-done((f32[4,128,512]{1,0,2:T(4,128)S(1)}, f32[4,128,512]{1,0,2:T(4,128)}, u32[]{:S(2)}, u32[]{:S(2)}) %collective-permute-start.1) | collective-permute-done | bytes 1048608 | tf_op jit(solution)/shard_map/ppermute | solution.py:16
  67.8 4.3 collective-permute-start.2
  74.6 14.3 %collective-permute-done.5 = f32[4,128,512]{1,0,2:T(4,128)} collective-permute-done((f32[4,128,512]{1,0,2:T(4,128)S(1)}, f32[4,128,512]{1,0,2:T(4,128)}, u32[]{:S(2)}, u32[]{:S(2)}) %collective-permute-start.5) | collective-permute-done | bytes 1048608 | tf_op jit(solution)/shard_map/ppermute | solution.py:16
  90.2 4.3 collective-permute-start.6
  94.5 16.8 %collective-permute-done.9 = f32[4,128,512]{1,0,2:T(4,128)} collective-permute-done((f32[4,128,512]{1,0,2:T(4,128)}, f32[4,128,512]{1,0,2:T(4,128)}, u32[]{:S(2)}, u32[]{:S(2)}) %collective-permute-start.9) | collective-permute-done | bytes 1048608 | tf_op jit(solution)/shard_map/ppermute | solution.py:16
  113.7 4.4 collective-permute-start.10
  118.2 13.6 %collective-permute-done.13 = f32[4,128,512]{1,0,2:T(4,128)} collective-permute-done((f32[4,128,512]{1,0,2:T(4,128)}, f32[4,128,512]{1,0,2:T(4,128)}, u32[]{:S(2)}, u32[]{:S(2)}) %collective-permute-start.13) | collective-permute-done | bytes 1048608 | tf_op jit(solution)/shard_map/ppermute | solution.py:16
  134.3 4.2 collective-permute-start.14
  148.6 19.5 %collective-permute-done.14 = f32[4,128,512]{1,0,2:T(4,128)} collective-permute-done((f32[4,128,512]{1,0,2:T(4,128)}, f32[4,128,512]{1,0,2:T(4,128)}, u32[]{:S(2)}, u32[]{:S(2)}) %collective-permute-start.14) | collective-permute-done | bytes 1048608 | tf_op jit(solution)/shard_map/ppermute | solution.py:16
  174.4 3.0 collective-permute-start.4
  186.9 7.0 collective-permute-done.7
  196.3 3.2 collective-permute-start.8
  199.5 16.9 %collective-permute-done.11 = f32[4,128,512]{1,0,2:T(4,128)} collective-permute-done((f32[4,128,512]{1,0,2:T(4,128)S(1)}, f32[4,128,512]{1,0,2:T(4,128)}, u32[]{:S(2)}, u32[]{:S(2)}) %collective-permute-start.11) | collective-permute-done | bytes 1048608 | tf_op jit(solution)/shard_map/ppermute | solution.py:16
  218.7 3.2 collective-permute-start.12
  221.9 16.9 %collective-permute-done.15 = f32[4,128,512]{1,0,2:T(4,128)} collective-permute-done((f32[4,128,512]{1,0,2:T(4,128)}, f32[4,128,512]{1,0,2:T(4,128)}, u32[]{:S(2)}, u32[]{:S(2)}) %collective-permute-start.15) | collective-permute-done | bytes 1048608 | tf_op jit(solution)/shard_map/ppermute | solution.py:16
  240.2 3.3 collective-permute-start.16
  243.5 20.3 %collective-permute-done.4 = f32[4,128,512]{1,0,2:T(4,128)} collective-permute-done((f32[4,128,512]{1,0,2:T(4,128)}, f32[4,128,512]{1,0,2:T(4,128)}, u32[]{:S(2)}, u32[]{:S(2)}) %collective-permute-start.4) | collective-permute-done | bytes 1048608 | tf_op jit(solution)/shard_map/ppermute | solution.py:16
  265.6 3.9 gather_fusion.2
  269.6 16.7 %collective-permute-done.8 = f32[4,128,512]{1,0,2:T(4,128)} collective-permute-done((f32[4,128,512]{1,0,2:T(4,128)}, f32[4,128,512]{1,0,2:T(4,128)}, u32[]{:S(2)}, u32[]{:S(2)}) %collective-permute-start.8) | collective-permute-done | bytes 1048608 | tf_op jit(solution)/shard_map/ppermute | solution.py:16
  288.1 4.0 gather_fusion.3
  292.1 16.7 %collective-permute-done.12 = f32[4,128,512]{1,0,2:T(4,128)} collective-permute-done((f32[4,128,512]{1,0,2:T(4,128)}, f32[4,128,512]{1,0,2:T(4,128)}, u32[]{:S(2)}, u32[]{:S(2)}) %collective-permute-start.12) | collective-permute-done | bytes 1048608 | tf_op jit(solution)/shard_map/ppermute | solution.py:16
  310.6 3.9 gather_fusion.4
  314.5 13.6 %collective-permute-done.16 = f32[4,128,512]{1,0,2:T(4,128)} collective-permute-done((f32[4,128,512]{1,0,2:T(4,128)S(1)}, f32[4,128,512]{1,0,2:T(4,128)}, u32[]{:S(2)}, u32[]{:S(2)}) %collective-permute-start.16) | collective-permute-done | bytes 1048608 | tf_op jit(solution)/shard_map/ppermute | solution.py:16
  329.9 12.6 %gather_fusion.5 = f32[4,128,512]{1,0,2:T(4,128)} fusion(f32[4,128,1024]{1,0,2:T(4,128)S(1)} %pad_maximum_fusion.3, s32[4]{0:T(128)S(1)} %fusion.121), kind=kCustom, calls=%fused_computation.3.clone | custom fusion | bytes 2097200 | tf_op jit(solution)/shard_map/vmap(jit(_roll_dynamic))/gather | solution.py:72
  342.6 7.1 convolution_bitcast_fusion.6
  349.8 5.2 convolution_bitcast_fusion.5
  355.1 5.2 convolution_bitcast_fusion.4
  360.4 5.5 fusion.9
  365.9 10.1 %all-reduce.1 = (f32[4,4]{1,0:T(4,128)S(1)}, f32[4,4,4]{1,2,0:T(4,128)S(1)}) all-reduce(f32[4,4]{1,0:T(4,128)S(1)} %fusion.9, f32[4,4,4]{1,2,0:T(4,128)S(1)} %bitcast.243), channel_id=1, replica_groups=mesh['sub'=32,'surf'=4] {'surf'}, use_global_device_ids=true, to_apply=%region_3.5 | all-reduce | flops 80 | bytes 640 | tf_op jit(solution)/shard_map/psum | solution.py:81
  382.1 4.8 fusion.102
  388.6 3.7 all-to-all-start
  392.7 23.0 %while.17 = (s32[]{:T(128)}, f32[1024,512]{1,0:T(8,128)}, s32[8,2]{0,1:T(2,128)S(1)}, f32[8,40,256]{2,1,0:T(8,128)S(1)}, s32[]{:T(128)}) while((s32[]{:T(128)}, f32[1024,512]{1,0:T(8,128)}, s32[8,2]{0,1:T(2,128)S(1)}, f32[8,40,256]{2,1,0:T(8,128)S(1)}, s32[]{:T(128)}) %tuple.88), condition=%wide.while_cond, body=%wide.while_body.sunk | while | flops 2 | bytes 82029 | solution.py:108
  417.5 5.3 fusion.41
  422.9 4.1 fusion.3
  430.2 113.9 %while.18 = (s32[]{:T(128)}, f32[1024,1024]{1,0:T(8,128)}, s32[2]{0:T(128)S(1)}, s32[2]{0:T(128)S(1)}, f32[4,2,40,256]{3,2,1,0:T(8,128)S(1)}, /*index=5*/s32[2]{...) while((s32[]{:T(128)}, f32[1024,1024]{1,0:T(8,128)}, ...), condition=%wide.region_11.13_spmd.clone, body=%wide.region_10.12_spmd.clone.sunk | while | flops 40993 | bytes 370382 | solution.py:136
  435.2 2.9 dynamic_update_slice.24
  441.6 2.9 dynamic_update_slice.25
  449.4 2.9 dynamic_update_slice.24
  455.9 2.9 dynamic_update_slice.25
  498.6 2.9 dynamic_update_slice.25
  512.8 2.9 dynamic_update_slice.25
  520.6 2.9 dynamic_update_slice.24
  544.8 190.4 %reduce-scatter.2.cloned.1.call-done = f32[32,1024]{1,0:T(8,128)} async-done(((f32[1024,1024]{1,0:T(8,128)}), f32[32,1024]{1,0:T(8,128)}) %reduce-scatter.2.cloned.1.call-update) | async-done | bytes 131088 | tf_op jit(solution)/shard_map/reduce_scatter | solution.py:137
  (235 shorter events, 147.3 us)
Async XLA Ops:
  7.2 3.4 copy-start.18
  7.2 9.1 %copy-start.22 = (s32[4,1]{0,1:T(1,128)S(1)}, s32[4,1]{0,1:T(1,128)}, u32[]{:S(2)}) copy-start(s32[4,1]{0,1:T(1,128)} %param.14) | copy-start | bytes 52
  7.2 9.3 %copy-start.19 = (s32[4,128]{1,0:T(4,128)S(1)}, s32[4,128]{1,0:T(4,128)}, u32[]{:S(2)}) copy-start(s32[4,128]{1,0:T(4,128)} %param.13) | copy-start | bytes 6148
  7.2 385.5 %all-gather.2.cloned.1.call-start = ((), (), s32[]{:S(2)}) async-start(), calls=%async_computation.2 | async-start | bytes 2162688 | tf_op jit(solution)/shard_map/all_gather | solution.py:98
  8.9 25.5 %copy-start.1 = (f32[4,128,512]{1,0,2:T(4,128)}, f32[4,128,512]{1,0,2:T(4,128)S(1)}, u32[]{:S(2)}) copy-start(f32[4,128,512]{1,0,2:T(4,128)S(1)} %copy.100) | copy-start | bytes 3145732
  8.9 25.5 %collective-permute-start = (f32[4,128,512]{1,0,2:T(4,128)S(1)}, f32[4,128,512]{1,0,2:T(4,128)}, u32[]{:S(2)}, u32[]{:S(2)}) collective-permute-start(f32[4,128,512]{1,0,2:T(4,128)S(1)} %copy.100), channel_id=1, source_target_pairs={{0,4},{4,0},{8,12},{12,8},{16,20},{20,16},{24,28},{28,24},{32,36},... | collective-permute-start | bytes 3145736 | tf_op jit(solution)/shard_map/ppermute | solution.py:16
  17.4 5.4 copy-start.9
  18.1 4.7 copy-start.11
  18.1 6.8 copy-start.20
  18.1 6.8 copy-start.21
  37.4 29.0 %copy-start.5 = (f32[8,128,256]{1,0,2:T(8,128)}, f32[8,128,256]{1,0,2:T(8,128)S(1)}, u32[]{:S(2)}) copy-start(f32[8,128,256]{1,0,2:T(8,128)S(1)} %get-tuple-element.280) | copy-start | bytes 3145732
  37.4 30.4 %copy-start.4 = (f32[8,128,256]{1,0,2:T(8,128)}, f32[8,128,256]{1,0,2:T(8,128)S(1)}, u32[]{:S(2)}) copy-start(f32[8,128,256]{1,0,2:T(8,128)S(1)} %get-tuple-element.283) | copy-start | bytes 3145732
  37.4 29.0 %collective-permute-start.1 = (f32[4,128,512]{1,0,2:T(4,128)S(1)}, f32[4,128,512]{1,0,2:T(4,128)}, u32[]{:S(2)}, u32[]{:S(2)}) collective-permute-start(f32[4,128,512]{1,0,2:T(4,128)S(1)} %bitcast.241), channel_id=1, source_target_pairs={{0,8},{8,0},{4,12},{12,4},{16,24},{24,16},{20,28},{28,20},{32,40},... | collective-permute-start | bytes 3145736 | tf_op jit(solution)/shard_map/ppermute | solution.py:16
  41.3 47.6 %collective-permute-start.5 = (f32[4,128,512]{1,0,2:T(4,128)S(1)}, f32[4,128,512]{1,0,2:T(4,128)}, u32[]{:S(2)}, u32[]{:S(2)}) collective-permute-start(f32[4,128,512]{1,0,2:T(4,128)S(1)} %bitcast.240), channel_id=1, source_target_pairs={{0,8},{8,0},{4,12},{12,4},{16,24},{24,16},{20,28},{28,20},{32,40},... | collective-permute-start | bytes 3145736 | tf_op jit(solution)/shard_map/ppermute | solution.py:16
  44.9 66.5 %collective-permute-start.9 = (f32[4,128,512]{1,0,2:T(4,128)}, f32[4,128,512]{1,0,2:T(4,128)}, u32[]{:S(2)}, u32[]{:S(2)}) collective-permute-start(f32[4,128,512]{1,0,2:T(4,128)} %bitcast.161), channel_id=1, source_target_pairs={{0,8},{8,0},{4,12},{12,4},{16,24},{24,16},{20,28},{28,20},{32,40},... | collective-permute-start | bytes 3145736 | tf_op jit(solution)/shard_map/ppermute | solution.py:16
  48.3 83.6 %collective-permute-start.13 = (f32[4,128,512]{1,0,2:T(4,128)}, f32[4,128,512]{1,0,2:T(4,128)}, u32[]{:S(2)}, u32[]{:S(2)}) collective-permute-start(f32[4,128,512]{1,0,2:T(4,128)} %bitcast.160), channel_id=1, source_target_pairs={{0,8},{8,0},{4,12},{12,4},{16,24},{24,16},{20,28},{28,20},{32,40},... | collective-permute-start | bytes 3145736 | tf_op jit(solution)/shard_map/ppermute | solution.py:16
  67.8 70.7 %collective-permute-start.2 = (f32[4,128,512]{1,0,2:T(4,128)S(1)}, f32[4,128,512]{1,0,2:T(4,128)}, u32[]{:S(2)}, u32[]{:S(2)}) collective-permute-start(f32[4,128,512]{1,0,2:T(4,128)S(1)} %bitcast.237), channel_id=1, source_target_pairs={{0,16},{16,0},{4,20},{20,4},{8,24},{24,8},{12,28},{28,12},{32,48},... | collective-permute-start | bytes 3145736 | tf_op jit(solution)/shard_map/ppermute | solution.py:16
  90.2 53.4 %collective-permute-start.6 = (f32[4,128,512]{1,0,2:T(4,128)S(1)}, f32[4,128,512]{1,0,2:T(4,128)}, u32[]{:S(2)}, u32[]{:S(2)}) collective-permute-start(f32[4,128,512]{1,0,2:T(4,128)S(1)} %bitcast.236), channel_id=1, source_target_pairs={{0,16},{16,0},{4,20},{20,4},{8,24},{24,8},{12,28},{28,12},{32,48},... | collective-permute-start | bytes 3145736 | tf_op jit(solution)/shard_map/ppermute | solution.py:16
  113.7 31.9 %collective-permute-start.10 = (f32[4,128,512]{1,0,2:T(4,128)}, f32[4,128,512]{1,0,2:T(4,128)}, u32[]{:S(2)}, u32[]{:S(2)}) collective-permute-start(f32[4,128,512]{1,0,2:T(4,128)} %bitcast.177), channel_id=1, source_target_pairs={{0,16},{16,0},{4,20},{20,4},{8,24},{24,8},{12,28},{28,12},{32,48},... | collective-permute-start | bytes 3145736 | tf_op jit(solution)/shard_map/ppermute | solution.py:16
  134.3 33.8 %collective-permute-start.14 = (f32[4,128,512]{1,0,2:T(4,128)}, f32[4,128,512]{1,0,2:T(4,128)}, u32[]{:S(2)}, u32[]{:S(2)}) collective-permute-start(f32[4,128,512]{1,0,2:T(4,128)} %bitcast.165), channel_id=1, source_target_pairs={{0,16},{16,0},{4,20},{20,4},{8,24},{24,8},{12,28},{28,12},{32,48},... | collective-permute-start | bytes 3145736 | tf_op jit(solution)/shard_map/ppermute | solution.py:16
  139.6 32.4 %collective-permute-start.3 = (f32[4,128,512]{1,0,2:T(4,128)}, f32[4,128,512]{1,0,2:T(4,128)}, u32[]{:S(2)}, u32[]{:S(2)}) collective-permute-start(f32[4,128,512]{1,0,2:T(4,128)} %bitcast.204), channel_id=1, source_target_pairs={{0,32},{32,0},{4,36},{36,4},{8,40},{40,8},{12,44},{44,12},{16,48},... | collective-permute-start | bytes 3145736 | tf_op jit(solution)/shard_map/ppermute | solution.py:16
  145.1 48.8 %collective-permute-start.7 = (f32[4,128,512]{1,0,2:T(4,128)S(1)}, f32[4,128,512]{1,0,2:T(4,128)}, u32[]{:S(2)}, u32[]{:S(2)}) collective-permute-start(f32[4,128,512]{1,0,2:T(4,128)S(1)} %bitcast.234), channel_id=1, source_target_pairs={{0,32},{32,0},{4,36},{36,4},{8,40},{40,8},{12,44},{44,12},{16,48},... | collective-permute-start | bytes 3145736 | tf_op jit(solution)/shard_map/ppermute | solution.py:16
  147.0 69.4 %collective-permute-start.11 = (f32[4,128,512]{1,0,2:T(4,128)S(1)}, f32[4,128,512]{1,0,2:T(4,128)}, u32[]{:S(2)}, u32[]{:S(2)}) collective-permute-start(f32[4,128,512]{1,0,2:T(4,128)S(1)} %bitcast.235), channel_id=1, source_target_pairs={{0,32},{32,0},{4,36},{36,4},{8,40},{40,8},{12,44},{44,12},{16,48},... | collective-permute-start | bytes 3145736 | tf_op jit(solution)/shard_map/ppermute | solution.py:16
  170.4 68.4 %collective-permute-start.15 = (f32[4,128,512]{1,0,2:T(4,128)}, f32[4,128,512]{1,0,2:T(4,128)}, u32[]{:S(2)}, u32[]{:S(2)}) collective-permute-start(f32[4,128,512]{1,0,2:T(4,128)} %bitcast.168), channel_id=1, source_target_pairs={{0,32},{32,0},{4,36},{36,4},{8,40},{40,8},{12,44},{44,12},{16,48},... | collective-permute-start | bytes 3145736 | tf_op jit(solution)/shard_map/ppermute | solution.py:16
  174.4 89.4 %collective-permute-start.4 = (f32[4,128,512]{1,0,2:T(4,128)}, f32[4,128,512]{1,0,2:T(4,128)}, u32[]{:S(2)}, u32[]{:S(2)}) collective-permute-start(f32[4,128,512]{1,0,2:T(4,128)} %bitcast.207), channel_id=1, source_target_pairs={{0,64},{64,0},{4,68},{68,4},{8,72},{72,8},{12,76},{76,12},{16,80},... | collective-permute-start | bytes 3145736 | tf_op jit(solution)/shard_map/ppermute | solution.py:16
  196.3 90.0 %collective-permute-start.8 = (f32[4,128,512]{1,0,2:T(4,128)}, f32[4,128,512]{1,0,2:T(4,128)}, u32[]{:S(2)}, u32[]{:S(2)}) collective-permute-start(f32[4,128,512]{1,0,2:T(4,128)} %bitcast.195), channel_id=1, source_target_pairs={{0,64},{64,0},{4,68},{68,4},{8,72},{72,8},{12,76},{76,12},{16,80},... | collective-permute-start | bytes 3145736 | tf_op jit(solution)/shard_map/ppermute | solution.py:16
  218.7 90.0 %collective-permute-start.12 = (f32[4,128,512]{1,0,2:T(4,128)}, f32[4,128,512]{1,0,2:T(4,128)}, u32[]{:S(2)}, u32[]{:S(2)}) collective-permute-start(f32[4,128,512]{1,0,2:T(4,128)} %bitcast.183), channel_id=1, source_target_pairs={{0,64},{64,0},{4,68},{68,4},{8,72},{72,8},{12,76},{76,12},{16,80},... | collective-permute-start | bytes 3145736 | tf_op jit(solution)/shard_map/ppermute | solution.py:16
  240.2 87.9 %collective-permute-start.16 = (f32[4,128,512]{1,0,2:T(4,128)S(1)}, f32[4,128,512]{1,0,2:T(4,128)}, u32[]{:S(2)}, u32[]{:S(2)}) collective-permute-start(f32[4,128,512]{1,0,2:T(4,128)S(1)} %bitcast.238), channel_id=1, source_target_pairs={{0,64},{64,0},{4,68},{68,4},{8,72},{72,8},{12,76},{76,12},{16,80},... | collective-permute-start | bytes 3145736 | tf_op jit(solution)/shard_map/ppermute | solution.py:16
  329.9 12.7 %copy-start.2 = (f32[4,128,512]{1,0,2:T(4,128)S(1)}, f32[4,128,512]{1,0,2:T(4,128)}, u32[]{:S(2)}) copy-start(f32[4,128,512]{1,0,2:T(4,128)} %copy-done.1) | copy-start | bytes 3145732
  342.6 7.1 copy-start.7
  342.6 7.1 copy-start.10
  342.6 7.2 copy-start.12
  342.6 7.2 copy-start.14
  349.8 5.3 copy-start.8
  349.8 5.3 copy-start.16
  355.0 5.3 copy-start.6
  355.1 5.3 copy-start.15
  360.3 19.3 %copy-start = (f32[4,128,512]{2,1,0:T(8,128)S(1)}, f32[4,128,512]{2,1,0:T(8,128)}, u32[]{:S(2)}) copy-start(f32[4,128,512]{2,1,0:T(8,128)} %param.11) | copy-start | bytes 3145732
  360.4 19.2 %copy-start.3 = (f32[4,128,512]{2,0,1:T(4,128)S(1)}, f32[4,128,512]{2,0,1:T(4,128)}, u32[]{:S(2)}) copy-start(f32[4,128,512]{2,0,1:T(4,128)} %copy.112) | copy-start | bytes 3145732
  388.6 4.1 copy-start.13
  388.6 34.3 %all-to-all-start = ((f32[4,2,128,512]{3,2,1,0:T(8,128)}), f32[4,2,128,512]{3,2,1,0:T(8,128)S(1)}, u32[]{:S(2)}, u32[]{:S(2)}) async-start(f32[4,2,128,512]{3,2,1,0:T(8,128)} %copy.114), calls=%async_computation | async-start | bytes 4194304 | tf_op jit(solution)/shard_map/all_to_all | solution.py:117
  392.3 342.9 %reduce-scatter.2.cloned.1.call-start = ((), (), s32[]{:S(2)}) async-start(), calls=%async_computation.3 | async-start | bytes 4325376 | tf_op jit(solution)/shard_map/reduce_scatter | solution.py:137
  544.1 191.1 %copy-start.17 = (f32[32,512]{1,0:T(8,128)S(1)}, f32[32,512]{1,0:T(8,128)}, u32[]{:S(2)}) copy-start(f32[32,512]{1,0:T(8,128)} %param.17) | copy-start | bytes 196612
Sparse Core Ops, SparseCore 0:
  11.1 161.2 all-gather.1
  544.3 190.9 reduce-scatter.1
where the time goes:
time: 759 us; the launch traced here: 744 us
  waiting for transfers between devices  389 us (51%)
  local copies, waits for them, and re-layouts  123 us (16%)
  other arithmetic  57.2 us (8%)
  matrix products  48.6 us (6%)
  starting transfers between devices  48.1 us (6%)
  loops' own time  38 us (5%)
  between operations  30 us (4%)
  blocking collectives  10.1 us (1%)
    ppermute x17, waiting for transfers between devices, partner(): return lax.ppermute(block, axis, route)  199 us
    reduce_scatter x1, waiting for transfers between devices, per_device(): summed = lax.psum_scatter(totals, 'sub', scatter_dimension=0, tiled=True)  190 us
    ppermute x17, starting transfers between devices, partner(): return lax.ppermute(block, axis, route)  44.1 us
    another operation x1, loops' own time, per_device(): totals = lax.fori_loop(0, n_surf * capacity, add_slot, totals)  37.9 us
    select_n x17, other arithmetic, per_device(): moving = jnp.where(masks[r] >> bit & 1 == 1, swapped, moving)  30.6 us
    gather x4, local copies, waits for them, and re-layouts, per_device(): jnp.roll(tile, k, axis=1)  24.5 us
    dot_general x4, matrix products, per_device(): jnp.einsum('kyx,jyx->jk', basis, jnp.tanh(0.5 * diff), precision=HIGH)  23.1 us
    gather x24, local copies, waits for them, and re-layouts  23 us
  transfers between devices with their start and end apart: 20, of which 14 were waited for; matrix products, arithmetic and copies ran while one was open for 19% of the time, Pallas kernels for 0%

commit v1 on v0

v1 whole, which is shorter than its diff:
```python
import functools

import jax
import jax.numpy as jnp
import ml_dtypes
import numpy as np
from jax import lax
from jax.experimental import pallas as pl
from jax.experimental.pallas import tpu as pltpu
from jax.sharding import PartitionSpec as P

HIGH = lax.Precision.HIGHEST
MESH = pl.DeviceIdType.MESH
F32 = jnp.float32
PIX = 512
ROUNDS = 4
SUBS = 128
N_SUB = 32
N_SURF = 4
WIN = 136
PART = 40
PAD = 32
TALL = WIN + 2 * PAD
BAND = 3


def spline_np(t):
    first = t**3 / 6.0
    second = (-3.0 * t**3 + 12.0 * t**2 - 12.0 * t + 4.0) / 6.0
    third = (3.0 * t**3 - 24.0 * t**2 + 60.0 * t - 44.0) / 6.0
    fourth = (4.0 - t) ** 3 / 6.0
    inner = np.where(t < 1, first, np.where(t < 2, second, np.where(t < 3, third, fourth)))
    return np.where((t < 0) | (t >= 4), 0.0, inner)


def table_np(rows, cols):
    return spline_np(np.arange(rows)[:, None] * 0.25 - np.arange(cols)[None, :] + 3.0)


COL_TABLE = np.rint(384 * table_np(PIX, 256)).astype(np.float32).astype(ml_dtypes.bfloat16)
ROW_TABLE_T = np.rint(384 * table_np(128, PART)).T.astype(np.float32).astype(ml_dtypes.bfloat16)

_FULL = table_np(PIX, 256)
_U = (np.arange(PIX) - 255.5) / 256.0
COL_NORMAL = (_FULL.T @ _FULL).astype(np.float32)
_NORMAL = _FULL.T @ _FULL
COL_SUMS = np.stack(
    [_FULL.T @ np.ones(PIX), _FULL.T @ _U, _FULL.T @ _U**2, np.diag(_NORMAL)]
).astype(np.float32)
COL_SUMS = np.concatenate([COL_SUMS, np.zeros((4, 256), np.float32)])
N_COEF = 131
_QUANT = np.zeros((N_COEF, 10))
for _a in range(N_COEF):
    for _d in range(-BAND, BAND + 1):
        if 0 <= _a + _d < N_COEF:
            _QUANT[_a, _d + BAND] = _NORMAL[_a, _a + _d]
_QUANT[:, 7:] = np.stack([_FULL.T @ np.ones(PIX), _FULL.T @ _U, _FULL.T @ _U**2], 1)[:N_COEF]
EDGES = (0, 1, 2, 128, 129, 130)
_ROW_U2 = [float((_U**k).sum()) for k in range(5)]
_MID = _QUANT[64]
_VAR = float(_MID[9] - 4.0 * ((4.0 * 63 - 255.5) / 256.0) ** 2)


def exact_dot(table, value):
    high = value.astype(jnp.bfloat16)
    low = (value - high.astype(F32)).astype(jnp.bfloat16)
    return jnp.dot(table, high, preferred_element_type=F32) + jnp.dot(
        table, low, preferred_element_type=F32
    )


def exact_dot_right(value, table):
    high = value.astype(jnp.bfloat16)
    low = (value - high.astype(F32)).astype(jnp.bfloat16)
    return jnp.dot(high, table, preferred_element_type=F32) + jnp.dot(
        low, table, preferred_element_type=F32
    )


def project_kernel(dest, h_ref, c_ref, r_ref, out_ref):
    out_ref[...] = jnp.zeros_like(out_ref)
    for j in range(4):
        wide = exact_dot_right(h_ref[j], c_ref[...])
        out_ref[dest[j]] = exact_dot(r_ref[...], wide) * (1.0 / (384.0 * 384.0))


def project(heights, dest):
    vmem = pl.BlockSpec(memory_space=pltpu.VMEM)
    return pl.pallas_call(
        project_kernel,
        out_shape=jax.ShapeDtypeStruct((8, PART, 256), F32),
        in_specs=[pl.BlockSpec(memory_space=pltpu.SMEM), vmem, vmem, vmem],
        out_specs=vmem,
        name="project",
    )(dest, heights, jnp.asarray(COL_TABLE), jnp.asarray(ROW_TABLE_T))


def gather_kernel(send_ref, meta_ref, tall_ref, metas_ref, parts, sems, own_sem):
    s, t = lax.axis_index("sub"), lax.axis_index("surf")
    x = s % 4
    base = s - x
    barrier = pltpu.get_barrier_semaphore()
    for k in range(1, 4):
        pl.semaphore_signal(
            barrier, inc=1, device_id={"sub": s, "surf": (t + k) % 4}, device_id_type=MESH
        )
        pl.semaphore_signal(
            barrier, inc=1, device_id={"sub": base + (x + k) % 4, "surf": t}, device_id_type=MESH
        )
    pl.semaphore_wait(barrier, 6)
    own = pltpu.make_async_copy(send_ref.at[t], parts.at[t], own_sem.at[0])
    own.start()
    own_meta = pltpu.make_async_copy(meta_ref, metas_ref.at[x], own_sem.at[1])
    own_meta.start()
    copies = []
    for k in range(1, 4):
        to = (t + k) % 4
        copy = pltpu.make_async_remote_copy(
            src_ref=send_ref.at[to],
            dst_ref=parts.at[t],
            send_sem=sems.at[0, k],
            recv_sem=sems.at[1, k],
            device_id={"sub": s, "surf": to},
            device_id_type=MESH,
        )
        copy.start()
        copies.append(copy)
        copy = pltpu.make_async_remote_copy(
            src_ref=meta_ref,
            dst_ref=metas_ref.at[x],
            send_sem=sems.at[2, k],
            recv_sem=sems.at[3, k],
            device_id={"sub": base + (x + k) % 4, "surf": t},
            device_id_type=MESH,
        )
        copy.start()
        copies.append(copy)
    for q in range(4):
        tall_ref[q, :, 0:PAD, :] = jnp.zeros((2, PAD, 256), F32)
        tall_ref[q, :, PAD + WIN : TALL, :] = jnp.zeros((2, PAD, 256), F32)
    own.wait()
    own_meta.wait()
    for copy in copies:
        copy.wait()
    tall_ref[x, :, PAD : PAD + WIN, :] = jnp.zeros((2, WIN, 256), F32)
    for p in range(4):
        rows = pl.ds(PAD + 32 * p, PART)
        tall_ref[x, :, rows, :] = tall_ref[x, :, rows, :] + parts[p]
    copies = []
    for k in range(1, 4):
        copy = pltpu.make_async_remote_copy(
            src_ref=tall_ref.at[x, :, pl.ds(PAD, WIN), :],
            dst_ref=tall_ref.at[x, :, pl.ds(PAD, WIN), :],
            send_sem=sems.at[4, k],
            recv_sem=sems.at[5, k],
            device_id={"sub": base + (x + k) % 4, "surf": t},
            device_id_type=MESH,
        )
        copy.start()
        copies.append(copy)
    for copy in copies:
        copy.wait()


def gather_windows(send, meta):
    vmem = pl.BlockSpec(memory_space=pltpu.VMEM)
    return pl.pallas_call(
        gather_kernel,
        out_shape=(
            jax.ShapeDtypeStruct((4, 2, TALL, 256), F32),
            jax.ShapeDtypeStruct((4, 1, 128), jnp.int32),
        ),
        in_specs=[vmem, vmem],
        out_specs=(vmem, vmem),
        scratch_shapes=[
            pltpu.VMEM((4, 2, PART, 256), F32),
            pltpu.SemaphoreType.DMA((6, 4)),
            pltpu.SemaphoreType.DMA((2,)),
        ],
        compiler_params=pltpu.CompilerParams(collective_id=0, has_side_effects=True),
        name="gather_windows",
    )(send.reshape(4, 2, PART, 256), meta)


def place_kernel(pos, tall_ref, out_ref):
    out_ref[...] = jnp.zeros_like(out_ref)
    x = pos[16]
    for w in range(8):
        start = pos[w]
        column = pl.multiple_of(pos[8 + w], 128)

        def one(b, carry, w=w, start=start, column=column):
            rel = 32 * (4 * b + x) - start

            @pl.when((rel > -32) & (rel < WIN))
            def _():
                first = rel + PAD
                base = pl.multiple_of(first // 8 * 8, 8)
                wide = tall_ref[pl.ds(w * TALL + base, 40), :]
                piece = pltpu.roll(wide, (40 - (first - base)) % 40, 0)[0:32]
                out_ref[b, :, pl.ds(column, 256)] = out_ref[b, :, pl.ds(column, 256)] + piece

            return carry

        lax.fori_loop(0, 8, one, 0)


def place(pos, tall):
    vmem = pl.BlockSpec(memory_space=pltpu.VMEM)
    return pl.pallas_call(
        place_kernel,
        out_shape=jax.ShapeDtypeStruct((8, 32, 512), F32),
        in_specs=[pl.BlockSpec(memory_space=pltpu.SMEM), vmem],
        out_specs=vmem,
        name="place",
    )(pos, tall.reshape(8 * TALL, 256))


def scatter_kernel(part_ref, surf_ref, back_ref, halo_ref, slots, sems, halo_sems):
    s, t = lax.axis_index("sub"), lax.axis_index("surf")
    x = s % 4
    b = s // 4
    up, down = (s + 1) % N_SUB, (s + N_SUB - 1) % N_SUB
    barrier = pltpu.get_barrier_semaphore()
    for k in range(1, 8):
        pl.semaphore_signal(
            barrier, inc=1, device_id={"sub": ((b + k) % 8) * 4 + x, "surf": t}, device_id_type=MESH
        )
    for to in (up, down):
        pl.semaphore_signal(barrier, inc=1, device_id={"sub": to, "surf": t}, device_id_type=MESH)
    pl.semaphore_wait(barrier, 9)
    copies = []
    for k in range(1, 8):
        to = (b + k) % 8
        copy = pltpu.make_async_remote_copy(
            src_ref=part_ref.at[to],
            dst_ref=slots.at[k],
            send_sem=sems.at[0, k],
            recv_sem=sems.at[1, k],
            device_id={"sub": to * 4 + x, "surf": t},
            device_id_type=MESH,
        )
        copy.start()
        copies.append(copy)
    for n, (to, first) in enumerate(((up, 24), (down, 0))):
        copy = pltpu.make_async_remote_copy(
            src_ref=surf_ref.at[pl.ds(first, 8), :],
            dst_ref=halo_ref.at[n],
            send_sem=halo_sems.at[0, n],
            recv_sem=halo_sems.at[1, n],
            device_id={"sub": to, "surf": t},
            device_id_type=MESH,
        )
        copy.start()
        copies.append(copy)
    for copy in copies:
        copy.wait()
    total = part_ref[b]
    for k in range(1, 8):
        total = total + slots[k]
    back_ref[...] = total


def scatter_sum(part, surface):
    vmem = pl.BlockSpec(memory_space=pltpu.VMEM)
    return pl.pallas_call(
        scatter_kernel,
        out_shape=(
            jax.ShapeDtypeStruct((32, 512), F32),
            jax.ShapeDtypeStruct((2, 8, 512), F32),
        ),
        in_specs=[vmem, vmem],
        out_specs=(vmem, vmem),
        scratch_shapes=[
            pltpu.VMEM((8, 32, 512), F32),
            pltpu.SemaphoreType.DMA((2, 8)),
            pltpu.SemaphoreType.DMA((2, 2)),
        ],
        compiler_params=pltpu.CompilerParams(collective_id=1, has_side_effects=True),
        name="scatter_sum",
    )(part, surface)


def moments_kernel(info, h_ref, recv_ref, out_ref):
    half, first_row, r = info[0], info[1], info[2]
    lower = half == 0
    xs = lax.broadcasted_iota(jnp.int32, (1, PIX), 1)
    ux = (xs.astype(F32) - 255.5) * (1.0 / 256.0)
    ys = lax.broadcasted_iota(jnp.int32, (64, 1), 0) + first_row
    uy = (ys.astype(F32) - 255.5) * (1.0 / 256.0)
    lanes = lax.broadcasted_iota(jnp.int32, (1, 128), 1)
    total = jnp.zeros((1, 128), F32)
    for j in range(4):
        shift = info[4 + j]
        padded = jnp.concatenate([recv_ref[j], jnp.zeros((64, 128), F32)], axis=1)
        moved = pltpu.roll(padded, info[8 + j], 1)
        low = jnp.where(lower, shift, 0)
        high = jnp.where(lower, PIX, PIX - shift)
        inside = (xs >= low) & (xs < high)
        value = jnp.where(inside, jnp.tanh(0.5 * (h_ref[j] - moved)), 0.0)
        value_y = value * uy
        sum0 = jnp.sum(value, axis=0, keepdims=True)
        sum1 = jnp.sum(value_y, axis=0, keepdims=True)
        sum2 = jnp.sum(value_y * uy, axis=0, keepdims=True)
        rows = (sum0, ux * sum0, sum1, ux * ux * sum0 + sum2)
        for k in range(4):
            total = jnp.where(
                lanes == 16 * j + 4 * r + k, jnp.sum(rows[k], axis=1, keepdims=True), total
            )
    out_ref[...] = total


def moments(info, heights, received):
    grid_spec = pltpu.PrefetchScalarGridSpec(
        num_scalar_prefetch=1,
        grid=(1,),
        in_specs=[
            pl.BlockSpec((4, 64, PIX), lambda i, info: (0, info[0], 0)),
            pl.BlockSpec((4, 64, 384), lambda i, info: (0, 0, 0)),
        ],
        out_specs=pl.BlockSpec((1, 128), lambda i, info: (0, 0)),
    )
    return pl.pallas_call(
        moments_kernel,
        out_shape=jax.ShapeDtypeStruct((1, 128), F32),
        grid_spec=grid_spec,
        name="moments",
    )(info, heights, received)


def share_kernel(row_ref, out_ref, parts, total, sems, far_sems, own_sem):
    s, t = lax.axis_index("sub"), lax.axis_index("surf")
    barrier = pltpu.get_barrier_semaphore()
    for k in range(1, 4):
        pl.semaphore_signal(
            barrier, inc=1, device_id={"sub": s, "surf": (t + k) % 4}, device_id_type=MESH
        )
    for k in range(1, N_SUB):
        pl.semaphore_signal(
            barrier, inc=1, device_id={"sub": (s + k) % N_SUB, "surf": t}, device_id_type=MESH
        )
    pl.semaphore_wait(barrier, 3 + N_SUB - 1)
    copies = []
    for k in range(1, 4):
        copy = pltpu.make_async_remote_copy(
            src_ref=row_ref,
            dst_ref=parts.at[k],
            send_sem=sems.at[0, k],
            recv_sem=sems.at[1, k],
            device_id={"sub": s, "surf": (t + k) % 4},
            device_id_type=MESH,
        )
        copy.start()
        copies.append(copy)
    for copy in copies:
        copy.wait()
    total[...] = (row_ref[...] + parts[1]) + (parts[2] + parts[3])
    own = pltpu.make_async_copy(total, out_ref.at[s], own_sem)
    own.start()
    copies = []
    for k in range(1, N_SUB):
        copy = pltpu.make_async_remote_copy(
            src_ref=total,
            dst_ref=out_ref.at[s],
            send_sem=far_sems.at[0, k],
            recv_sem=far_sems.at[1, k],
            device_id={"sub": (s + k) % N_SUB, "surf": t},
            device_id_type=MESH,
        )
        copy.start()
        copies.append(copy)
    own.wait()
    for copy in copies:
        copy.wait()


def share(row):
    vmem = pl.BlockSpec(memory_space=pltpu.VMEM)
    return pl.pallas_call(
        share_kernel,
        out_shape=jax.ShapeDtypeStruct((N_SUB, 1, 128), F32),
        in_specs=[vmem],
        out_specs=vmem,
        scratch_shapes=[
            pltpu.VMEM((4, 1, 128), F32),
            pltpu.VMEM((1, 128), F32),
            pltpu.SemaphoreType.DMA((2, 4)),
            pltpu.SemaphoreType.DMA((2, N_SUB)),
            pltpu.SemaphoreType.DMA,
        ],
        compiler_params=pltpu.CompilerParams(collective_id=2, has_side_effects=True),
        name="share",
    )(row)


def swap_lanes(value, width, bit, lanes):
    swapped = jnp.where(
        (lanes & width) != 0,
        pltpu.roll(value, width, 1),
        pltpu.roll(value, 128 - width, 1),
    )
    return jnp.where(bit == 1, swapped, value)


def finish_kernel(info, off_ref, m_ref, s_ref, back_ref, halo_ref, gc_ref, cs_ref, par_ref, out_ref):
    me, section = info[0], info[1]
    lane1 = lax.broadcasted_iota(jnp.int32, (1, 128), 1)
    sub1 = lane1 // 4
    rows16 = lax.broadcasted_iota(jnp.int32, (16, 128), 0)
    lane16 = lax.broadcasted_iota(jnp.int32, (16, 128), 1)
    mask16 = jnp.zeros((16, 128), jnp.int32)
    for r in range(ROUNDS):
        mask16 = jnp.where(rows16 // 4 == r, info[2 + r], mask16)
    spread = (
        lax.broadcasted_iota(jnp.int32, (N_SUB, 128), 1) // 4
        == lax.broadcasted_iota(jnp.int32, (N_SUB, 128), 0)
    ).astype(F32)
    table = lax.dot_general(
        m_ref[:, 0, :], spread, (((0,), (0,)), ((), ())), precision=HIGH, preferred_element_type=F32
    )
    own = jnp.zeros((16, 128), F32)
    place = jnp.zeros((8, 128), F32)
    for j in range(4):
        own = jnp.where(lane16 % 4 == j, table[16 * j : 16 * j + 16], own)
        place = jnp.where(lane16[:8] % 4 == j, table[64 + 8 * j : 72 + 8 * j], place)
    other = own
    shifts = off_ref[...]
    mask4 = jnp.concatenate([mask16[4 * r : 4 * r + 1] for r in range(ROUNDS)], axis=0)
    lane4 = lane16[:4]
    other_shift = shifts
    for bit in range(5):
        other = swap_lanes(other, 4 << bit, (mask16 >> bit) & 1, lane16)
        other_shift = swap_lanes(other_shift, 4 << bit, (mask4 >> bit) & 1, lane4)
    lower4 = (lane4 // 4) < jnp.bitwise_xor(lane4 // 4, mask4)
    shifts = jnp.where(lower4, shifts, other_shift)
    delta = jnp.where(lower4, shifts, -shifts).astype(F32) * (1.0 / 256.0)
    rhs = [jnp.zeros((1, 128), F32) for _ in range(4)]
    for r in range(ROUNDS):
        o = [own[4 * r + k : 4 * r + k + 1] for k in range(4)]
        p = [other[4 * r + k : 4 * r + k + 1] for k in range(4)]
        d = delta[r : r + 1]
        rhs[0] = rhs[0] + (o[0] - p[0])
        rhs[1] = rhs[1] + (o[1] - (p[1] + d * p[0]))
        rhs[2] = rhs[2] + (o[2] - p[2])
        rhs[3] = rhs[3] + (o[3] - (p[3] + d * (2.0 * p[1] + d * p[0])))
    column = lax.broadcasted_iota(jnp.int32, (PIX, 128), 0)
    count = jnp.zeros((PIX, 128), F32)
    for r in range(ROUNDS):
        shift = shifts[r : r + 1]
        low = jnp.where(lower4[r : r + 1], shift, 0)
        high = jnp.where(lower4[r : r + 1], PIX, PIX - shift)
        count = count + jnp.where((column >= low) & (column < high), 1.0, 0.0)
    ux = (lax.broadcasted_iota(jnp.int32, (PIX, 1), 0).astype(F32) - 255.5) * (1.0 / 256.0)
    power = []
    term = count
    for k in range(5):
        power.append(jnp.sum(term, axis=0, keepdims=True))
        if k < 4:
            term = term * ux
    y0, y2, y4 = _ROW_U2[0], _ROW_U2[2], _ROW_U2[4]
    g00 = power[0] * y0
    g01 = power[1] * y0
    g03 = power[2] * y0 + power[0] * y2
    g11 = power[2] * y0
    g13 = power[3] * y0 + power[1] * y2
    g22 = power[0] * y2
    g33 = power[4] * y0 + 2.0 * power[2] * y2 + power[0] * y4
    l00 = jnp.sqrt(g00)
    l10 = g01 / l00
    l30 = g03 / l00
    l11 = jnp.sqrt(g11 - l10 * l10)
    l31 = (g13 - l30 * l10) / l11
    l33 = jnp.sqrt(g33 - l30 * l30 - l31 * l31)
    z0 = rhs[0] / l00
    z1 = (rhs[1] - l10 * z0) / l11
    z3 = (rhs[3] - l30 * z0 - l31 * z1) / l33
    p3 = z3 / l33
    p1 = (z1 - l31 * p3) / l11
    p0 = (z0 - l10 * p1 - l30 * p3) / l00
    p2 = rhs[2] / g22
    params = jnp.concatenate([p0, p1, p2, p3], axis=0)
    par_ref[...] = pltpu.roll(params, (128 - 4 * me) % 128, 1)[:, 0:4]
    start = place[1:2].astype(jnp.int32)
    a = lax.broadcasted_iota(jnp.int32, (32, 128), 0) + 32 * me - start
    in_window = (a >= 0) & (a < N_COEF)
    middle = (a > EDGES[2]) & (a < EDGES[3])
    edges = [(a == e).astype(F32) for e in EDGES]

    def quantity(q, inner):
        value = jnp.where(middle, inner, 0.0)
        for e, at in zip(EDGES, edges):
            if _QUANT[e, q] != 0.0:
                value = value + at * float(_QUANT[e, q])
        return value

    centre = (4.0 * (a.astype(F32) - 1.0) - 255.5) * (1.0 / 256.0)
    bands = [quantity(q, float(_MID[q])) for q in range(7)]
    sum0 = quantity(7, 4.0)
    sum1 = quantity(8, 4.0 * centre)
    sum2 = quantity(9, 4.0 * centre * centre + _VAR)
    plane0 = p0 * sum0 + p2 * sum1 + p3 * sum2
    plane1 = p1 * sum0
    plane2 = p3 * sum0
    out_ref[...] = back_ref[...]
    weight = [jnp.zeros((32, 128), F32) for _ in range(4)]
    for c in range(3):
        chosen = (place[0:1] == section.astype(F32)) & (place[2:3] == float(c))
        chosen = chosen.astype(F32)
        band = [jnp.sum(v * chosen, axis=1, keepdims=True) for v in bands]
        plane = [jnp.sum(v * chosen, axis=1, keepdims=True) for v in (plane0, plane1, plane2)]
        cols = pl.ds(128 * c, 256)
        tall = jnp.concatenate([halo_ref[0, :, cols], s_ref[:, cols], halo_ref[1, :, cols]], axis=0)
        normal = jnp.dot(tall, gc_ref[...], precision=HIGH, preferred_element_type=F32)
        taken = plane[0] * cs_ref[0:1] + plane[1] * cs_ref[1:2] + plane[2] * cs_ref[2:3]
        for d in range(-BAND, BAND + 1):
            taken = taken + band[d + BAND] * normal[8 + d : 40 + d]
        out_ref[:, cols] = out_ref[:, cols] - taken
        diag = band[BAND] * cs_ref[3:4]
        weight[c] = weight[c] + diag[:, :128]
        weight[c + 1] = weight[c + 1] + diag[:, 128:]
    for c in range(4):
        cols = pl.ds(128 * c, 128)
        out_ref[:, cols] = s_ref[:, cols] + out_ref[:, cols] / (weight[c] + 1.0)


def finish(info, offsets, shared, surface, back, halo):
    vmem = pl.BlockSpec(memory_space=pltpu.VMEM)
    return pl.pallas_call(
        finish_kernel,
        out_shape=(jax.ShapeDtypeStruct((4, 4), F32), jax.ShapeDtypeStruct((32, 512), F32)),
        in_specs=[pl.BlockSpec(memory_space=pltpu.SMEM)] + [vmem] * 7,
        out_specs=(vmem, vmem),
        name="finish",
    )(info, offsets, shared, surface, back, halo, jnp.asarray(COL_NORMAL), jnp.asarray(COL_SUMS))


def swap_with(mask, block):
    return lax.ppermute(block, "sub", [(s, s ^ mask) for s in range(N_SUB)])


def per_device(heights, masks, offsets, sections, row_starts, col_blocks, surface):
    me_sub = lax.axis_index("sub")
    me_surf = lax.axis_index("surf")
    local = jnp.arange(4, dtype=jnp.int32)
    section_of = sections[:, 0]
    earlier = (section_of[:, None] == section_of[None, :]) & (local[None, :] < local[:, None])
    slot_of = jnp.sum(earlier.astype(jnp.int32), axis=1)
    dest = section_of * 2 + slot_of

    send = project(heights, dest)
    own_slot = (dest[None, :] == me_surf * 2 + jnp.arange(2, dtype=jnp.int32)[:, None]).astype(jnp.int32)
    slot_row = jnp.sum(own_slot * row_starts[None, :], axis=1)
    slot_col = jnp.sum(own_slot * col_blocks[None, :], axis=1) * 128
    meta = jnp.concatenate([slot_row, slot_col, jnp.zeros((124,), jnp.int32)])[None, :]
    tall, metas = gather_windows(send, meta)
    pos = jnp.concatenate(
        [metas[:, 0, 0:2].reshape(8), metas[:, 0, 2:4].reshape(8), (me_sub % 4)[None]]
    )
    part = place(pos, tall)
    back, halo = scatter_sum(part, surface)

    branches = [functools.partial(swap_with, m) for m in range(1, N_SUB)]

    def one_round(r, row):
        mask = masks[r]
        other = jnp.bitwise_xor(me_sub, mask)
        lower = me_sub < other
        half = jnp.where(lower, 0, 1)
        block = lax.dynamic_slice(heights, (0, 64 * (1 - half), 128 * (1 - half)), (4, 64, 384))
        received = lax.switch(mask - 1, branches, block)
        shift = lax.dynamic_slice(offsets, (r, jnp.minimum(me_sub, other) * 4), (1, 4))[0]
        turn = jnp.where(lower, shift, (640 - shift) % 512)
        info = jnp.concatenate(
            [jnp.stack([half, me_surf * 128 + 64 * half, r, r]), shift, turn]
        ).astype(jnp.int32)
        return row + moments(info, heights, received)

    row = lax.fori_loop(0, ROUNDS, one_round, jnp.zeros((1, 128), F32))
    places = jnp.stack([section_of, row_starts, col_blocks] + [jnp.zeros((4,), jnp.int32)] * 5, axis=1)
    places = jnp.where(me_surf == 0, places, 0).astype(F32).reshape(32)
    row = row + jnp.pad(places, (64, 32))[None, :]
    shared = share(row)
    info = jnp.concatenate([jnp.stack([me_sub, me_surf]), masks]).astype(jnp.int32)
    params, fitted = finish(info, offsets, shared, surface, back, halo)
    return params, fitted


def solution(mesh):
    in_specs = (
        P("sub", "surf", None),
        P(),
        P(),
        P("sub", None),
        P("sub"),
        P("sub"),
        P("sub", "surf"),
    )
    out_specs = (P(None, "sub"), P("sub", "surf"))
    return jax.shard_map(
        per_device, mesh=mesh, in_specs=in_specs, out_specs=out_specs, check_vma=False
    )
```

time: 759 us -> 147 us (0.19); the launches traced: 744 us -> 146 us
  waiting for transfers between devices: 389 us -> 33.4 us
  local copies, waits for them, and re-layouts: 123 us -> 6.84 us
  Pallas kernels: 0 us -> 77.8 us
  other arithmetic: 57.2 us -> 7.82 us
  matrix products: 48.6 us -> 0 us
  starting transfers between devices: 48.1 us -> 14.1 us
  loops' own time: 38 us -> 5.12 us
  between operations: 30 us -> 0.76 us
  blocking collectives: 10.1 us -> 0 us
    reduce_scatter x1 -> x0, waiting for transfers between devices: 190 us -> none  [per_device(): summed = lax.psum_scatter(totals, 'sub', scatter_dimension=0, tiled=True)]
    ppermute x17 -> x4, waiting for transfers between devices: 199 us -> 33.4 us  [swap_with(): return lax.ppermute(block, 'sub', [(s, s ^ mask) for s in range(N_SUB)])]
    pallas_call x0 -> x10, Pallas kernels: none -> 77.8 us  [the longest x1 25.4 us: gather_windows(): pl.pallas_call(gather_kernel, out_shape=(jax.ShapeDtypeStruct((4, 2, TALL...]
    gather x30 -> x0, local copies, waits for them, and re-layouts: 48.7 us -> none  [the longest x4 24.5 us: per_device(): jnp.roll(tile, k, axis=1)]
    dot_general x15 -> x0, matrix products: 48.2 us -> none  [the longest x4 23.1 us: per_device(): jnp.einsum('kyx,jyx->jk', basis, jnp.tanh(0.5 * diff), precision=HIGH)]
    dynamic_update_slice x16 -> x0, local copies, waits for them, and re-layouts: 45.7 us -> none  [the longest x8 22.9 us: add_slot(): lax.dynamic_update_slice(total, old_diag + scaled, (ystart, sec_cols + xs...]
    another operation x2 -> x5, loops' own time: 38 us -> 5.12 us  [the longest x1 5 us: per_device(): row = lax.fori_loop(0, ROUNDS, one_round, jnp.zeros((1, 128), F32))]
    select_n x19 -> x4, other arithmetic: 30.7 us -> 0.33 us  [one_round(): turn = jnp.where(lower, shift, (640 - shift) % 512)]
  transfers between devices with their start and end apart: 20 -> 4, of which waited for: 14 -> 4; matrix products, arithmetic and copies ran while one was open for 19% -> 0% of each run, Pallas kernels for 0% -> 0%
where the time goes in v1:
time: 147 us; the launch traced here: 146 us
  Pallas kernels  77.8 us (53%)
  waiting for transfers between devices  33.4 us (23%)
  starting transfers between devices  14.1 us (10%)
  other arithmetic  7.82 us (5%)
  local copies, waits for them, and re-layouts  6.84 us (5%)
  loops' own time  5.12 us (3%)
    ppermute x4, waiting for transfers between devices, swap_with(): return lax.ppermute(block, 'sub', [(s, s ^ mask) for s in range(N_SUB)])  33.4 us
    pallas_call x1, Pallas kernels, gather_windows(): pl.pallas_call(gather_kernel, out_shape=(jax.ShapeDtypeStruct((4, 2, TALL...  25.4 us
    pallas_call x1, Pallas kernels, share(): pl.pallas_call(share_kernel, out_shape=jax.ShapeDtypeStruct((N_SUB, 1, 12...  16.3 us
    pallas_call x1, Pallas kernels, scatter_sum(): pl.pallas_call(scatter_kernel, out_shape=(jax.ShapeDtypeStruct((32, 512),...  15.7 us
    ppermute x4, starting transfers between devices, swap_with(): return lax.ppermute(block, 'sub', [(s, s ^ mask) for s in range(N_SUB)])  14.1 us
    pallas_call x4, Pallas kernels, moments(): pl.pallas_call(moments_kernel, out_shape=jax.ShapeDtypeStruct((1, 128), F...  10.8 us
    another operation x1, loops' own time, per_device(): row = lax.fori_loop(0, ROUNDS, one_round, jnp.zeros((1, 128), F32))  5 us
    pallas_call x1, Pallas kernels, place(): pl.pallas_call(place_kernel, out_shape=jax.ShapeDtypeStruct((8, 32, 512),...  3.48 us
  transfers between devices with their start and end apart: 4, of which 4 were waited for; matrix products, arithmetic and copies ran while one was open for 0% of the time, Pallas kernels for 0%

profile of v1, /device:TPU:0, one launch (start us, length us, event | category | flops | bytes accessed | tf_op | source)
XLA Modules:
  0.0 145.9 jit_solution(9049661266925177928)
XLA Ops:
  0.7 0.9 convert_reduce_fusion
  1.6 0.7 multiply_add_fusion.dest
  2.2 0.9 fusion.3
  3.1 0.6 add_bitcast_fusion.meta_ref
  3.8 3.2 %project.1 = f32[8,40,256]{2,1,0:T(8,128)} custom-call(s32[4]{0:T(128)} %copy-done.2, f32[4,128,512]{2,1,0:T(8,128)} %h_ref.1, bf16[512,256]{1,0:T(8,128)(2,1)} %constant.140.clone.c_ref, bf16[40,128]{1,0:T(8,128)(2,1)} %constant.141.clone.r_ref), custom_call_target="tpu_custom_call" | custom-call | tf_op jit(solution)/shard_map/project/pallas_call | solution.py:89
  7.0 25.4 %gather_windows.1 = (f32[4,2,200,256]{3,2,1,0:T(8,128)}, s32[4,1,128]{2,1,0:T(1,128)}) custom-call(f32[4,2,40,256]{3,2,1,0:T(8,128)} %bitcast.29, s32[1,128]{1,0:T(1,128)} %add_bitcast_fusion.meta_ref), custom_call_target="tpu_custom_call" | custom-call | tf_op jit(solution)/shard_map/gather_windows/pallas_call | solution.py:167
  32.4 0.8 slice_reduce_fusion.1
  33.4 0.7 pad_add_fusion.1.pos
  34.1 3.5 %place.1.part_ref = f32[8,32,512]{2,1,0:T(8,128)} custom-call(s32[17]{0:T(128)} %pad_add_fusion.1.pos, f32[1600,256]{1,0:T(8,128)} %bitcast.28), custom_call_target="tpu_custom_call" | custom-call | tf_op jit(solution)/shard_map/place/pallas_call | solution.py:210
  37.6 15.7 %scatter_sum.1 = (f32[32,512]{1,0:T(8,128)}, f32[2,8,512]{2,1,0:T(8,128)}) custom-call(f32[8,32,512]{2,1,0:T(8,128)} %place.1.part_ref, f32[32,512]{1,0:T(8,128)} %s_ref.1), custom_call_target="tpu_custom_call" | custom-call | tf_op jit(solution)/shard_map/scatter_sum/pallas_call | solution.py:266
  53.3 71.6 %while.16 = (s32[]{:T(128)}, f32[1,128]{1,0:T(1,128)S(1)}, s32[4]{0:T(128)S(1)}, s32[]{:T(128)}, s32[]{:T(128)}, /*index=5*/s32[4,128]{1,0:T(4,128)S(1)}, f32[4,...) while((s32[]{:T(128)}, f32[1,128]{1,0:T(1,128)S(1)}, ...), condition=%wide.region_32.33_spmd.clone, body=%wide.region_0.32_spmd.clone.sunk | while | flops 332 | bytes 2361452 | solution.py:578
  53.3 0.6 dynamic_slice.132
  55.2 12.4 %conditional.3 = (f32[4,64,384]{2,1,0:T(8,128)}) conditional(s32[]{:T(128)} %clamp.12, f32[4,64,384]{2,1,0:T(8,128)S(1)} %constant_dynamic-slice_fusion.2, f32[4,64,384]{2,1,0:T(8,128)S(1)} %constant_dynamic-slice_fusion.2, f32[4,64,384]{2,1,0:T(8,128)S(1)} %constant_dynamic-slice_fusion.2, ...), branch_computations={%region_1.1_spmd, %region_2.2_spmd, %region_3.3_spmd, %region_4.4_... | conditional | bytes 1572912 | solution.py:570
  55.3 1.8 %collective-permute-start.9 = (f32[4,64,384]{2,1,0:T(8,128)S(1)}, f32[4,64,384]{2,1,0:T(8,128)}, u32[]{:S(2)}, u32[]{:S(2)}) collective-permute-start(f32[4,64,384]{2,1,0:T(8,128)S(1)} %param.9), channel_id=1, source_target_pairs={{0,40},{4,44},{8,32},{12,36},{16,56},{20,60},{24,48},{28,52},{32,8... | collective-permute-start | bytes 1179656 | tf_op jit(solution)/shard_map/while/body/eval_jaxpr/cond/branch_9_fun/ppermute | solution.py:538
  57.0 10.6 %collective-permute-done.9 = f32[4,64,384]{2,1,0:T(8,128)} collective-permute-done((f32[4,64,384]{2,1,0:T(8,128)S(1)}, f32[4,64,384]{2,1,0:T(8,128)}, u32[]{:S(2)}, u32[]{:S(2)}) %collective-permute-start.9) | collective-permute-done | bytes 393248 | tf_op jit(solution)/shard_map/while/body/eval_jaxpr/cond/branch_9_fun/ppermute | solution.py:538
  67.7 0.7 concatenate.17.info
  68.4 2.7 %moments.8 = f32[1,128]{1,0:T(1,128)} custom-call(s32[12]{0:T(128)} %concatenate.17.info, f32[4,128,512]{2,1,0:T(8,128)S(1)} %get-tuple-element.379.h_ref, f32[4,64,384]{2,1,0:T(8,128)} %get-tuple-element.388.recv_ref), custom_call_target="tpu_custom_call" | custom-call | tf_op jit(solution)/shard_map/while/body/eval_jaxpr/moments/pallas_call | solution.py:323
  71.1 0.6 fusion.6
  71.7 0.6 dynamic_slice.132
  73.6 10.6 %conditional.3 = (f32[4,64,384]{2,1,0:T(8,128)}) conditional(s32[]{:T(128)} %clamp.12, f32[4,64,384]{2,1,0:T(8,128)S(1)} %constant_dynamic-slice_fusion.2, f32[4,64,384]{2,1,0:T(8,128)S(1)} %constant_dynamic-slice_fusion.2, f32[4,64,384]{2,1,0:T(8,128)S(1)} %constant_dynamic-slice_fusion.2, ...), branch_computations={%region_1.1_spmd, %region_2.2_spmd, %region_3.3_spmd, %region_4.4_... | conditional | bytes 1572912 | solution.py:570
  73.6 2.7 %collective-permute-start.15 = (f32[4,64,384]{2,1,0:T(8,128)S(1)}, f32[4,64,384]{2,1,0:T(8,128)}, u32[]{:S(2)}, u32[]{:S(2)}) collective-permute-start(f32[4,64,384]{2,1,0:T(8,128)S(1)} %param.15), channel_id=1, source_target_pairs={{0,64},{4,68},{8,72},{12,76},{16,80},{20,84},{24,88},{28,92},{32,9... | collective-permute-start | bytes 1179656 | tf_op jit(solution)/shard_map/while/body/eval_jaxpr/cond/branch_15_fun/ppermute | solution.py:538
  76.3 8.0 %collective-permute-done.15 = f32[4,64,384]{2,1,0:T(8,128)} collective-permute-done((f32[4,64,384]{2,1,0:T(8,128)S(1)}, f32[4,64,384]{2,1,0:T(8,128)}, u32[]{:S(2)}, u32[]{:S(2)}) %collective-permute-start.15) | collective-permute-done | bytes 393248 | tf_op jit(solution)/shard_map/while/body/eval_jaxpr/cond/branch_15_fun/ppermute | solution.py:538
  84.3 0.7 concatenate.17.info
  85.0 2.7 %moments.8 = f32[1,128]{1,0:T(1,128)} custom-call(s32[12]{0:T(128)} %concatenate.17.info, f32[4,128,512]{2,1,0:T(8,128)S(1)} %get-tuple-element.379.h_ref, f32[4,64,384]{2,1,0:T(8,128)} %get-tuple-element.388.recv_ref), custom_call_target="tpu_custom_call" | custom-call | tf_op jit(solution)/shard_map/while/body/eval_jaxpr/moments/pallas_call | solution.py:323
  87.7 0.6 fusion.6
  88.3 0.6 dynamic_slice.132
  90.2 8.3 %conditional.3 = (f32[4,64,384]{2,1,0:T(8,128)}) conditional(s32[]{:T(128)} %clamp.12, f32[4,64,384]{2,1,0:T(8,128)S(1)} %constant_dynamic-slice_fusion.2, f32[4,64,384]{2,1,0:T(8,128)S(1)} %constant_dynamic-slice_fusion.2, f32[4,64,384]{2,1,0:T(8,128)S(1)} %constant_dynamic-slice_fusion.2, ...), branch_computations={%region_1.1_spmd, %region_2.2_spmd, %region_3.3_spmd, %region_4.4_... | conditional | bytes 1572912 | solution.py:570
  90.2 0.1 collective-permute-start
  90.3 8.2 %collective-permute-done = f32[4,64,384]{2,1,0:T(8,128)} collective-permute-done((f32[4,64,384]{2,1,0:T(8,128)S(1)}, f32[4,64,384]{2,1,0:T(8,128)}, u32[]{:S(2)}, u32[]{:S(2)}) %collective-permute-start) | collective-permute-done | bytes 393248 | tf_op jit(solution)/shard_map/while/body/eval_jaxpr/cond/branch_0_fun/ppermute | solution.py:538
  98.6 0.7 concatenate.17.info
  99.2 2.7 %moments.8 = f32[1,128]{1,0:T(1,128)} custom-call(s32[12]{0:T(128)} %concatenate.17.info, f32[4,128,512]{2,1,0:T(8,128)S(1)} %get-tuple-element.379.h_ref, f32[4,64,384]{2,1,0:T(8,128)} %get-tuple-element.388.recv_ref), custom_call_target="tpu_custom_call" | custom-call | tf_op jit(solution)/shard_map/while/body/eval_jaxpr/moments/pallas_call | solution.py:323
  101.9 0.6 fusion.6
  102.5 0.6 dynamic_slice.132
  104.4 16.4 %conditional.3 = (f32[4,64,384]{2,1,0:T(8,128)}) conditional(s32[]{:T(128)} %clamp.12, f32[4,64,384]{2,1,0:T(8,128)S(1)} %constant_dynamic-slice_fusion.2, f32[4,64,384]{2,1,0:T(8,128)S(1)} %constant_dynamic-slice_fusion.2, f32[4,64,384]{2,1,0:T(8,128)S(1)} %constant_dynamic-slice_fusion.2, ...), branch_computations={%region_1.1_spmd, %region_2.2_spmd, %region_3.3_spmd, %region_4.4_... | conditional | bytes 1572912 | solution.py:570
  104.5 9.6 %collective-permute-start.30 = (f32[4,64,384]{2,1,0:T(8,128)S(1)}, f32[4,64,384]{2,1,0:T(8,128)}, u32[]{:S(2)}, u32[]{:S(2)}) collective-permute-start(f32[4,64,384]{2,1,0:T(8,128)S(1)} %param.30), channel_id=1, source_target_pairs={{0,124},{4,120},{8,116},{12,112},{16,108},{20,104},{24,100},{28,96... | collective-permute-start | bytes 1179656 | tf_op jit(solution)/shard_map/while/body/eval_jaxpr/cond/branch_30_fun/ppermute | solution.py:538
  114.1 6.7 %collective-permute-done.30 = f32[4,64,384]{2,1,0:T(8,128)} collective-permute-done((f32[4,64,384]{2,1,0:T(8,128)S(1)}, f32[4,64,384]{2,1,0:T(8,128)}, u32[]{:S(2)}, u32[]{:S(2)}) %collective-permute-start.30) | collective-permute-done | bytes 393248 | tf_op jit(solution)/shard_map/while/body/eval_jaxpr/cond/branch_30_fun/ppermute | solution.py:538
  120.9 0.7 concatenate.17.info
  121.6 2.7 %moments.8 = f32[1,128]{1,0:T(1,128)} custom-call(s32[12]{0:T(128)} %concatenate.17.info, f32[4,128,512]{2,1,0:T(8,128)S(1)} %get-tuple-element.379.h_ref, f32[4,64,384]{2,1,0:T(8,128)} %get-tuple-element.388.recv_ref), custom_call_target="tpu_custom_call" | custom-call | tf_op jit(solution)/shard_map/while/body/eval_jaxpr/moments/pallas_call | solution.py:323
  124.3 0.6 fusion.6
  124.9 0.1 copy.19
  125.0 0.1 copy.20
  125.1 0.1 copy.21
  125.2 0.1 stack.50
  125.3 0.1 convert_element_type.14
  125.4 0.6 bitcast_add_fusion.row_ref
  126.0 16.3 %share.1.m_ref = f32[32,1,128]{2,1,0:T(1,128)} custom-call(f32[1,128]{1,0:T(1,128)} %bitcast_add_fusion.row_ref), custom_call_target="tpu_custom_call" | custom-call | tf_op jit(solution)/shard_map/share/pallas_call | solution.py:379
  142.3 0.7 pad_add_fusion.info
  143.0 2.9 %finish.1 = (f32[4,4]{1,0:T(4,128)}, f32[32,512]{1,0:T(8,128)}) custom-call(s32[6]{0:T(128)} %pad_add_fusion.info, s32[4,128]{1,0:T(4,128)S(1)} %get-tuple-element.420, f32[32,1,128]{2,1,0:T(1,128)} %share.1.m_ref, f32[32,512]{1,0:T(8,128)} %s_ref.1, f32[32,512]{1,0:T(8,128)} %get-tuple-element.250.back_ref, f32[2,8,512]{2,1,0:T(8,128)} %get-tuple-element.251.halo_ref, ...), custom_call_target="tpu_custom_call" | custom-call | tf_op jit(solution)/shard_map/finish/pallas_call | solution.py:528
  (31 shorter events, 0.7 us)
Async XLA Ops:
  2.2 1.5 %copy-start.2 = (s32[4]{0:T(128)}, s32[4]{0:T(128)S(1)}, u32[]{:S(2)}) copy-start(s32[4]{0:T(128)S(1)} %multiply_add_fusion.dest) | copy-start | bytes 52
  7.0 46.2 %copy-start = (f32[4,128,512]{2,1,0:T(8,128)S(1)}, f32[4,128,512]{2,1,0:T(8,128)}, u32[]{:S(2)}) copy-start(f32[4,128,512]{2,1,0:T(8,128)} %h_ref.1) | copy-start | bytes 3145732
  7.0 46.2 %copy-start.1 = (s32[4,128]{1,0:T(4,128)S(1)}, s32[4,128]{1,0:T(4,128)}, u32[]{:S(2)}) copy-start(s32[4,128]{1,0:T(4,128)} %off_ref.1) | copy-start | bytes 6148
  7.0 46.3 %copy-start.6 = (s32[4]{0:T(128)S(1)}, s32[4]{0:T(128)}, u32[]{:S(2)}) copy-start(s32[4]{0:T(128)} %param.45) | copy-start | bytes 52
  53.3 71.6 %copy-start.5 = (s32[4,1]{0,1:T(1,128)S(1)}, s32[4,1]{0,1:T(1,128)}, u32[]{:S(2)}) copy-start(s32[4,1]{0,1:T(1,128)} %param.47) | copy-start | bytes 52
  53.3 71.7 %copy-start.3 = (s32[4]{0:T(128)S(1)}, s32[4]{0:T(128)}, u32[]{:S(2)}) copy-start(s32[4]{0:T(128)} %param.48) | copy-start | bytes 52
  53.3 71.8 %copy-start.4 = (s32[4]{0:T(128)S(1)}, s32[4]{0:T(128)}, u32[]{:S(2)}) copy-start(s32[4]{0:T(128)} %param.49) | copy-start | bytes 52
  55.3 12.4 %collective-permute-start.9 = (f32[4,64,384]{2,1,0:T(8,128)S(1)}, f32[4,64,384]{2,1,0:T(8,128)}, u32[]{:S(2)}, u32[]{:S(2)}) collective-permute-start(f32[4,64,384]{2,1,0:T(8,128)S(1)} %param.9), channel_id=1, source_target_pairs={{0,40},{4,44},{8,32},{12,36},{16,56},{20,60},{24,48},{28,52},{32,8... | collective-permute-start | bytes 1179656 | tf_op jit(solution)/shard_map/while/body/eval_jaxpr/cond/branch_9_fun/ppermute | solution.py:538
  73.6 10.6 %collective-permute-start.15 = (f32[4,64,384]{2,1,0:T(8,128)S(1)}, f32[4,64,384]{2,1,0:T(8,128)}, u32[]{:S(2)}, u32[]{:S(2)}) collective-permute-start(f32[4,64,384]{2,1,0:T(8,128)S(1)} %param.15), channel_id=1, source_target_pairs={{0,64},{4,68},{8,72},{12,76},{16,80},{20,84},{24,88},{28,92},{32,9... | collective-permute-start | bytes 1179656 | tf_op jit(solution)/shard_map/while/body/eval_jaxpr/cond/branch_15_fun/ppermute | solution.py:538
  90.2 8.3 %collective-permute-start = (f32[4,64,384]{2,1,0:T(8,128)S(1)}, f32[4,64,384]{2,1,0:T(8,128)}, u32[]{:S(2)}, u32[]{:S(2)}) collective-permute-start(f32[4,64,384]{2,1,0:T(8,128)S(1)} %param), channel_id=1, source_target_pairs={{0,4},{4,0},{8,12},{12,8},{16,20},{20,16},{24,28},{28,24},{32,36},... | collective-permute-start | bytes 1179656 | tf_op jit(solution)/shard_map/while/body/eval_jaxpr/cond/branch_0_fun/ppermute | solution.py:538
  104.5 16.3 %collective-permute-start.30 = (f32[4,64,384]{2,1,0:T(8,128)S(1)}, f32[4,64,384]{2,1,0:T(8,128)}, u32[]{:S(2)}, u32[]{:S(2)}) collective-permute-start(f32[4,64,384]{2,1,0:T(8,128)S(1)} %param.30), channel_id=1, source_target_pairs={{0,124},{4,120},{8,116},{12,112},{16,108},{20,104},{24,100},{28,96... | collective-permute-start | bytes 1179656 | tf_op jit(solution)/shard_map/while/body/eval_jaxpr/cond/branch_30_fun/ppermute | solution.py:538

commit v2 on v1

--- a/solution.py
+++ b/solution.py
@@ -1,5 +1,3 @@
-import functools
-
 import jax
 import jax.numpy as jnp
 import ml_dtypes
@@ -281,116 +279,172 @@
     )(part, surface)
 
 
-def moments_kernel(info, h_ref, recv_ref, out_ref):
-    half, first_row, r = info[0], info[1], info[2]
-    lower = half == 0
-    xs = lax.broadcasted_iota(jnp.int32, (1, PIX), 1)
-    ux = (xs.astype(F32) - 255.5) * (1.0 / 256.0)
-    ys = lax.broadcasted_iota(jnp.int32, (64, 1), 0) + first_row
-    uy = (ys.astype(F32) - 255.5) * (1.0 / 256.0)
-    lanes = lax.broadcasted_iota(jnp.int32, (1, 128), 1)
-    total = jnp.zeros((1, 128), F32)
-    for j in range(4):
-        shift = info[4 + j]
-        padded = jnp.concatenate([recv_ref[j], jnp.zeros((64, 128), F32)], axis=1)
-        moved = pltpu.roll(padded, info[8 + j], 1)
-        low = jnp.where(lower, shift, 0)
-        high = jnp.where(lower, PIX, PIX - shift)
-        inside = (xs >= low) & (xs < high)
-        value = jnp.where(inside, jnp.tanh(0.5 * (h_ref[j] - moved)), 0.0)
-        value_y = value * uy
-        sum0 = jnp.sum(value, axis=0, keepdims=True)
-        sum1 = jnp.sum(value_y, axis=0, keepdims=True)
-        sum2 = jnp.sum(value_y * uy, axis=0, keepdims=True)
-        rows = (sum0, ux * sum0, sum1, ux * ux * sum0 + sum2)
-        for k in range(4):
-            total = jnp.where(
-                lanes == 16 * j + 4 * r + k, jnp.sum(rows[k], axis=1, keepdims=True), total
-            )
-    out_ref[...] = total
-
-
-def moments(info, heights, received):
-    grid_spec = pltpu.PrefetchScalarGridSpec(
-        num_scalar_prefetch=1,
-        grid=(1,),
-        in_specs=[
-            pl.BlockSpec((4, 64, PIX), lambda i, info: (0, info[0], 0)),
-            pl.BlockSpec((4, 64, 384), lambda i, info: (0, 0, 0)),
-        ],
-        out_specs=pl.BlockSpec((1, 128), lambda i, info: (0, 0)),
-    )
-    return pl.pallas_call(
-        moments_kernel,
-        out_shape=jax.ShapeDtypeStruct((1, 128), F32),
-        grid_spec=grid_spec,
-        name="moments",
-    )(info, heights, received)
-
-
-def share_kernel(row_ref, out_ref, parts, total, sems, far_sems, own_sem):
+STAGES = 5
+
+
+def hop(s, kind):
+    if kind == 0:
+        return s + 1 - 2 * (s % 2)
+    if kind == 1:
+        return s + 3 - 2 * (s % 4)
+    if kind == 2:
+        return s + 4 - 8 * ((s // 4) % 2)
+    if kind == 3:
+        return s + 8 - 16 * ((s // 8) % 2)
+    return s + 24 - 16 * (s // 8)
+
+
+def taken(mask, kind):
+    bit = [(mask >> n) & 1 for n in range(5)]
+    return (bit[0] + bit[1]) % 2 if kind == 0 else (
+        (bit[3] + bit[4]) % 2 if kind == 3 else bit[{1: 1, 2: 2, 4: 4}[kind]]
+    )
+
+
+def rounds_kernel(turns, info_ref, h_ref, place_ref, out_ref, pay, recv, parts, total, sems, near_sems, far_sems, own_sem):
     s, t = lax.axis_index("sub"), lax.axis_index("surf")
     barrier = pltpu.get_barrier_semaphore()
     for k in range(1, 4):
         pl.semaphore_signal(
             barrier, inc=1, device_id={"sub": s, "surf": (t + k) % 4}, device_id_type=MESH
         )
-    for k in range(1, N_SUB):
+    for kind in range(5):
         pl.semaphore_signal(
-            barrier, inc=1, device_id={"sub": (s + k) % N_SUB, "surf": t}, device_id_type=MESH
-        )
-    pl.semaphore_wait(barrier, 3 + N_SUB - 1)
+            barrier, inc=1, device_id={"sub": hop(s, kind), "surf": t}, device_id_type=MESH
+        )
+
+    def flag(row, width):
+        return info_ref[row : row + 1, 0:width] == 1
+
+    def first(j, carry):
+        for r in range(ROUNDS):
+            pay[0, r, j] = jnp.where(flag(r, 384), h_ref[j, 64:128, 128:512], h_ref[j, 0:64, 0:384])
+        return carry
+
+    lax.fori_loop(0, 4, first, 0)
+    pl.semaphore_wait(barrier, 8)
+
+    def copy_of(k, r, j):
+        return pltpu.make_async_remote_copy(
+            src_ref=pay.at[k, r, j],
+            dst_ref=recv.at[k, r, j],
+            send_sem=sems.at[0, k, r, j],
+            recv_sem=sems.at[1, k, r, j],
+            device_id={"sub": hop(s, (k + r) % 5), "surf": t},
+            device_id_type=MESH,
+        )
+
+    def begin(j, carry):
+        for r in range(ROUNDS):
+            copy_of(0, r, j).start()
+        return carry
+
+    lax.fori_loop(0, 4, begin, 0)
+    for k in range(STAGES - 1):
+
+        def forward(j, carry, k=k):
+            for r in range(ROUNDS):
+                copy_of(k, r, j).wait_recv()
+                pay[k + 1, r, j] = jnp.where(
+                    flag(4 + 4 * k + r, 384), recv[k, r, j], pay[k, r, j]
+                )
+            for r in range(ROUNDS):
+                copy_of(k + 1, r, j).start()
+            return carry
+
+        lax.fori_loop(0, 4, forward, 0)
+
+    xs = lax.broadcasted_iota(jnp.int32, (1, PIX), 1)
+    ux = (xs.astype(F32) - 255.5) * (1.0 / 256.0)
+    lanes = lax.broadcasted_iota(jnp.int32, (1, 128), 1)
+    k = STAGES - 1
+
+    def last(j, row):
+        for r in range(ROUNDS):
+            lower = flag(r, PIX)
+            ys = lax.broadcasted_iota(jnp.int32, (64, 1), 0) + (128 * t + 64)
+            uy = ((ys - 64 * info_ref[r : r + 1, 0:1]).astype(F32) - 255.5) * (1.0 / 256.0)
+            copy_of(k, r, j).wait_recv()
+            came = jnp.where(flag(4 + 4 * k + r, 384), recv[k, r, j], pay[k, r, j])
+            shift = info_ref[pl.ds(24 + 4 * j + r, 1), :]
+            padded = jnp.concatenate([came, jnp.zeros((64, 128), F32)], axis=1)
+            moved = pltpu.roll(padded, turns[4 * r + j], 1)
+            inside = jnp.where(lower, xs - shift, PIX - 1 - shift - xs) >= 0
+            own = jnp.where(lower, h_ref[j, 0:64], h_ref[j, 64:128])
+            value = jnp.where(inside, jnp.tanh(0.5 * (own - moved)), 0.0)
+            value_y = value * uy
+            sum0 = jnp.sum(value, axis=0, keepdims=True)
+            sum1 = jnp.sum(value_y, axis=0, keepdims=True)
+            sum2 = jnp.sum(value_y * uy, axis=0, keepdims=True)
+            rows = (sum0, ux * sum0, sum1, ux * ux * sum0 + sum2)
+            for q in range(4):
+                row = jnp.where(
+                    lanes == 16 * j + 4 * r + q, jnp.sum(rows[q], axis=1, keepdims=True), row
+                )
+        return row
+
+    total[0] = lax.fori_loop(0, 4, last, place_ref[...])
     copies = []
-    for k in range(1, 4):
+    for n in range(1, 4):
         copy = pltpu.make_async_remote_copy(
-            src_ref=row_ref,
-            dst_ref=parts.at[k],
-            send_sem=sems.at[0, k],
-            recv_sem=sems.at[1, k],
-            device_id={"sub": s, "surf": (t + k) % 4},
+            src_ref=total.at[0],
+            dst_ref=parts.at[n],
+            send_sem=near_sems.at[0, n],
+            recv_sem=near_sems.at[1, n],
+            device_id={"sub": s, "surf": (t + n) % 4},
             device_id_type=MESH,
         )
         copy.start()
         copies.append(copy)
+
+    def settle(j, carry):
+        for k in range(STAGES):
+            for r in range(ROUNDS):
+                copy_of(k, r, j).wait_send()
+        return carry
+
+    lax.fori_loop(0, 4, settle, 0)
     for copy in copies:
         copy.wait()
-    total[...] = (row_ref[...] + parts[1]) + (parts[2] + parts[3])
-    own = pltpu.make_async_copy(total, out_ref.at[s], own_sem)
+    total[1] = (total[0] + parts[1]) + (parts[2] + parts[3])
+    own = pltpu.make_async_copy(total.at[1], out_ref.at[s], own_sem)
     own.start()
-    copies = []
-    for k in range(1, N_SUB):
-        copy = pltpu.make_async_remote_copy(
-            src_ref=total,
+
+    def far(n):
+        return pltpu.make_async_remote_copy(
+            src_ref=total.at[1],
             dst_ref=out_ref.at[s],
-            send_sem=far_sems.at[0, k],
-            recv_sem=far_sems.at[1, k],
-            device_id={"sub": (s + k) % N_SUB, "surf": t},
-            device_id_type=MESH,
-        )
-        copy.start()
-        copies.append(copy)
+            send_sem=far_sems.at[0, n],
+            recv_sem=far_sems.at[1, n],
+            device_id={"sub": (s + n) % N_SUB, "surf": t},
+            device_id_type=MESH,
+        )
+
+    lax.fori_loop(1, N_SUB, lambda n, c: (far(n).start(), c)[1], 0)
     own.wait()
-    for copy in copies:
-        copy.wait()
-
-
-def share(row):
+    lax.fori_loop(1, N_SUB, lambda n, c: (far(n).wait(), c)[1], 0)
+
+
+def rounds(turns, info, heights, places):
     vmem = pl.BlockSpec(memory_space=pltpu.VMEM)
     return pl.pallas_call(
-        share_kernel,
+        rounds_kernel,
         out_shape=jax.ShapeDtypeStruct((N_SUB, 1, 128), F32),
-        in_specs=[vmem],
+        in_specs=[pl.BlockSpec(memory_space=pltpu.SMEM), vmem, vmem, vmem],
         out_specs=vmem,
         scratch_shapes=[
+            pltpu.VMEM((STAGES, ROUNDS, 4, 64, 384), F32),
+            pltpu.VMEM((STAGES, ROUNDS, 4, 64, 384), F32),
             pltpu.VMEM((4, 1, 128), F32),
-            pltpu.VMEM((1, 128), F32),
+            pltpu.VMEM((2, 1, 128), F32),
+            pltpu.SemaphoreType.DMA((2, STAGES, ROUNDS, 4)),
             pltpu.SemaphoreType.DMA((2, 4)),
             pltpu.SemaphoreType.DMA((2, N_SUB)),
             pltpu.SemaphoreType.DMA,
         ],
         compiler_params=pltpu.CompilerParams(collective_id=2, has_side_effects=True),
-        name="share",
-    )(row)
+        name="rounds",
+    )(turns, info, heights, places)
 
 
 def swap_lanes(value, width, bit, lanes):
@@ -534,10 +588,6 @@
     )(info, offsets, shared, surface, back, halo, jnp.asarray(COL_NORMAL), jnp.asarray(COL_SUMS))
 
 
-def swap_with(mask, block):
-    return lax.ppermute(block, "sub", [(s, s ^ mask) for s in range(N_SUB)])
-
-
 def per_device(heights, masks, offsets, sections, row_starts, col_blocks, surface):
     me_sub = lax.axis_index("sub")
     me_surf = lax.axis_index("surf")
@@ -559,27 +609,19 @@
     part = place(pos, tall)
     back, halo = scatter_sum(part, surface)
 
-    branches = [functools.partial(swap_with, m) for m in range(1, N_SUB)]
-
-    def one_round(r, row):
-        mask = masks[r]
-        other = jnp.bitwise_xor(me_sub, mask)
-        lower = me_sub < other
-        half = jnp.where(lower, 0, 1)
-        block = lax.dynamic_slice(heights, (0, 64 * (1 - half), 128 * (1 - half)), (4, 64, 384))
-        received = lax.switch(mask - 1, branches, block)
-        shift = lax.dynamic_slice(offsets, (r, jnp.minimum(me_sub, other) * 4), (1, 4))[0]
-        turn = jnp.where(lower, shift, (640 - shift) % 512)
-        info = jnp.concatenate(
-            [jnp.stack([half, me_surf * 128 + 64 * half, r, r]), shift, turn]
-        ).astype(jnp.int32)
-        return row + moments(info, heights, received)
-
-    row = lax.fori_loop(0, ROUNDS, one_round, jnp.zeros((1, 128), F32))
+    other = jnp.bitwise_xor(me_sub, masks)
+    lower = me_sub < other
+    pair = jnp.minimum(me_sub, other)[:, None] * 4 + local[None, :]
+    shift = jnp.take_along_axis(offsets, pair, axis=1)
+    turn = jnp.where(lower[:, None], shift, (640 - shift) % 512)
+    used = jnp.stack(
+        [taken(masks[r], (k + r) % 5) for k in range(STAGES) for r in range(ROUNDS)]
+    )
+    steps = jnp.concatenate([lower.astype(jnp.int32), used, shift.T.reshape(16)])
+    steps = jnp.broadcast_to(steps[:, None], (40, PIX))
     places = jnp.stack([section_of, row_starts, col_blocks] + [jnp.zeros((4,), jnp.int32)] * 5, axis=1)
     places = jnp.where(me_surf == 0, places, 0).astype(F32).reshape(32)
-    row = row + jnp.pad(places, (64, 32))[None, :]
-    shared = share(row)
+    shared = rounds(turn.reshape(16), steps, heights, jnp.pad(places, (64, 32))[None, :])
     info = jnp.concatenate([jnp.stack([me_sub, me_surf]), masks]).astype(jnp.int32)
     params, fitted = finish(info, offsets, shared, surface, back, halo)
     return params, fitted

time: 147 us -> 133 us (0.905)
  waiting for transfers between devices: 33.4 us -> 0 us
  Pallas kernels: 77.8 us -> 107 us
  starting transfers between devices: 14.1 us -> 0 us
  between operations: 0.76 us -> 13.4 us
  loops' own time: 5.12 us -> 0 us
    pallas_call x5 -> x1, Pallas kernels: 27.1 us -> 60.6 us  [rounds(): pl.pallas_call(rounds_kernel, out_shape=jax.ShapeDtypeStruct((N_SUB, 1, 1...]
    ppermute x4 -> x0, waiting for transfers between devices: 33.4 us -> none  [swap_with(): return lax.ppermute(block, 'sub', [(s, s ^ mask) for s in range(N_SUB)])]
    ppermute x4 -> x0, starting transfers between devices: 14.1 us -> none  [swap_with(): return lax.ppermute(block, 'sub', [(s, s ^ mask) for s in range(N_SUB)])]
    another operation x5 -> x0, loops' own time: 5.12 us -> none  [the longest x1 5 us: per_device(): row = lax.fori_loop(0, ROUNDS, one_round, jnp.zeros((1, 128), F32))]
    add x5 -> x0, other arithmetic: 3.03 us -> none  [the longest x4 2.44 us: one_round(): return row + moments(info, heights, received)]
    dynamic_slice x8 -> x0, local copies, waits for them, and re-layouts: 2.63 us -> none  [the longest x4 2.47 us: one_round(): mask = masks[r]]
    concatenate x4 -> x1, local copies, waits for them, and re-layouts: 2.72 us -> 0.1 us  [per_device(): jnp.concatenate([lower.astype(jnp.int32), used, shift.T.reshape(16)])]
    pallas_call x1, Pallas kernels: 25.4 us -> 22.9 us  [gather_windows(): pl.pallas_call(gather_kernel, out_shape=(jax.ShapeDtypeStruct((4, 2, TALL...]
  transfers between devices with their start and end apart: 4 -> 0, of which waited for: 4 -> 0; matrix products, arithmetic and copies ran while one was open for 0% -> 0% of each run, Pallas kernels for 0% -> 0%
where the time goes in v2:
time: 133 us
  Pallas kernels  107 us (80%)
  between operations  13.4 us (10%)
  other arithmetic  6.95 us (5%)
  local copies, waits for them, and re-layouts  5.48 us (4%)
    pallas_call x1, Pallas kernels, rounds(): pl.pallas_call(rounds_kernel, out_shape=jax.ShapeDtypeStruct((N_SUB, 1, 1...  60.6 us
    pallas_call x1, Pallas kernels, gather_windows(): pl.pallas_call(gather_kernel, out_shape=(jax.ShapeDtypeStruct((4, 2, TALL...  22.9 us
    pallas_call x1, Pallas kernels, scatter_sum(): pl.pallas_call(scatter_kernel, out_shape=(jax.ShapeDtypeStruct((32, 512),...  14 us
    pallas_call x1, Pallas kernels, place(): pl.pallas_call(place_kernel, out_shape=jax.ShapeDtypeStruct((8, 32, 512),...  3.54 us
    pallas_call x1, Pallas kernels, project(): pl.pallas_call(project_kernel, out_shape=jax.ShapeDtypeStruct((8, PART, 2...  3.22 us
    pallas_call x1, Pallas kernels, finish(): pl.pallas_call(finish_kernel, out_shape=(jax.ShapeDtypeStruct((4, 4), F32...  2.88 us

profile of v2, /device:TPU:0, one launch (start us, length us, event | category | flops | bytes accessed | tf_op | source)
XLA Modules:
  0.0 132.9 jit_solution(13554617008953814390)
XLA Ops:
  0.6 0.0 copy-start
  0.6 0.0 copy-start.4
  0.7 0.0 copy-start.3
  0.7 0.0 copy-start.2
  0.7 1.3 pad_add_fusion.info
  2.0 0.7 minimum_multiply_fusion
  2.6 0.9 convert_reduce_fusion
  3.5 0.7 multiply_add_fusion.dest
  4.2 0.0 copy-start.1
  4.2 0.9 fusion.7
  5.1 0.6 add_bitcast_fusion.meta_ref
  5.7 0.7 fusion.11
  6.4 0.1 broadcast_in_dim.24
  6.5 0.1 broadcast_in_dim.42
  6.5 0.1 fusion.2
  6.6 0.1 reshape.203
  6.7 1.4 %gather_fusion = s32[16]{0:T(128)S(1)} fusion(s32[4,128]{1,0:T(4,128)} %off_ref.1, s32[16]{0:T(128)S(1)} %reshape.203), kind=kCustom, calls=%fused_computation | custom fusion | bytes 256 | tf_op jit(solution)/shard_map/jit(take_along_axis)/gather | solution.py:615
  8.1 0.1 reshape.206
  8.2 0.1 bitcast_select_fusion
  8.2 0.1 copy.17
  8.3 0.1 reshape.200
  8.4 0.1 add.160
  8.5 0.1 add.161
  8.6 0.0 copy-done.4
  8.6 0.0 copy-done.3
  8.6 0.0 copy-done.2
  8.6 0.1 copy.18
  8.7 0.1 convert_element_type.18
  8.8 0.7 pad_bitcast_fusion.place_ref
  9.5 0.1 add.163
  9.6 0.5 fusion.9.turns
  10.1 0.0 copy-done
  10.1 0.7 fusion.12
  23.4 0.1 concatenate.13
  23.5 0.7 broadcast_in_dim.43.info_ref
  24.2 60.6 %rounds.1.m_ref = f32[32,1,128]{2,1,0:T(1,128)} custom-call(s32[16]{0:T(128)} %fusion.9.turns, s32[40,512]{1,0:T(8,128)} %broadcast_in_dim.43.info_ref, f32[4,128,512]{2,1,0:T(8,128)} %h_ref.3, f32[1,128]{1,0:T(1,128)} %pad_bitcast_fusion.place_ref), custom_call_target="tpu_custom_call" | custom-call | tf_op jit(solution)/shard_map/rounds/pallas_call | solution.py:430
  84.7 0.0 copy-done.1
  84.8 3.2 %project.1 = f32[8,40,256]{2,1,0:T(8,128)} custom-call(s32[4]{0:T(128)} %copy-done.1, f32[4,128,512]{2,1,0:T(8,128)} %h_ref.3, bf16[512,256]{1,0:T(8,128)(2,1)} %constant.157.clone.c_ref, bf16[40,128]{1,0:T(8,128)(2,1)} %constant.158.clone.r_ref), custom_call_target="tpu_custom_call" | custom-call | tf_op jit(solution)/shard_map/project/pallas_call | solution.py:87
  88.0 22.9 %gather_windows.1 = (f32[4,2,200,256]{3,2,1,0:T(8,128)}, s32[4,1,128]{2,1,0:T(1,128)}) custom-call(f32[4,2,40,256]{3,2,1,0:T(8,128)} %bitcast.36, s32[1,128]{1,0:T(1,128)} %add_bitcast_fusion.meta_ref), custom_call_target="tpu_custom_call" | custom-call | tf_op jit(solution)/shard_map/gather_windows/pallas_call | solution.py:165
  110.9 0.8 slice_reduce_fusion.1
  111.7 0.1 reshape_squeeze.6
  111.8 0.1 reshape_squeeze.7
  111.9 0.6 pad_add_fusion.1.pos
  112.5 3.5 %place.1.part_ref = f32[8,32,512]{2,1,0:T(8,128)} custom-call(s32[17]{0:T(128)} %pad_add_fusion.1.pos, f32[1600,256]{1,0:T(8,128)} %bitcast.35), custom_call_target="tpu_custom_call" | custom-call | tf_op jit(solution)/shard_map/place/pallas_call | solution.py:208
  116.0 14.0 %scatter_sum.1 = (f32[32,512]{1,0:T(8,128)}, f32[2,8,512]{2,1,0:T(8,128)}) custom-call(f32[8,32,512]{2,1,0:T(8,128)} %place.1.part_ref, f32[32,512]{1,0:T(8,128)} %s_ref.1), custom_call_target="tpu_custom_call" | custom-call | tf_op jit(solution)/shard_map/scatter_sum/pallas_call | solution.py:264
  130.0 2.9 %finish.1 = (f32[4,4]{1,0:T(4,128)}, f32[32,512]{1,0:T(8,128)}) custom-call(s32[6]{0:T(128)} %pad_add_fusion.info, s32[4,128]{1,0:T(4,128)} %off_ref.1, f32[32,1,128]{2,1,0:T(1,128)} %rounds.1.m_ref, f32[32,512]{1,0:T(8,128)} %s_ref.1, f32[32,512]{1,0:T(8,128)} %get-tuple-element.8.back_ref, f32[2,8,512]{2,1,0:T(8,128)} %get-tuple-element.9.halo_ref, ...), custom_call_target="tpu_custom_call" | custom-call | tf_op jit(solution)/shard_map/finish/pallas_call | solution.py:582
  (8 shorter events, 0.1 us)
Async XLA Ops:
  0.6 9.5 %copy-start = (s32[4]{0:T(128)S(1)}, s32[4]{0:T(128)}, u32[]{:S(2)}) copy-start(s32[4]{0:T(128)} %param.12) | copy-start | bytes 52
  0.6 7.9 %copy-start.4 = (s32[4,1]{0,1:T(1,128)S(1)}, s32[4,1]{0,1:T(1,128)}, u32[]{:S(2)}) copy-start(s32[4,1]{0,1:T(1,128)} %param.14) | copy-start | bytes 52
  0.7 7.9 %copy-start.3 = (s32[4]{0:T(128)S(1)}, s32[4]{0:T(128)}, u32[]{:S(2)}) copy-start(s32[4]{0:T(128)} %param.16) | copy-start | bytes 52
  0.7 7.9 %copy-start.2 = (s32[4]{0:T(128)S(1)}, s32[4]{0:T(128)}, u32[]{:S(2)}) copy-start(s32[4]{0:T(128)} %param.15) | copy-start | bytes 52
  4.2 80.5 %copy-start.1 = (s32[4]{0:T(128)}, s32[4]{0:T(128)S(1)}, u32[]{:S(2)}) copy-start(s32[4]{0:T(128)S(1)} %multiply_add_fusion.dest) | copy-start | bytes 52

commit v3 on v2

v3 whole, which is shorter than its diff:
```python
import jax
import jax.numpy as jnp
import ml_dtypes
import numpy as np
from jax import lax
from jax.experimental import pallas as pl
from jax.experimental.pallas import tpu as pltpu
from jax.sharding import PartitionSpec as P

HIGH = lax.Precision.HIGHEST
MESH = pl.DeviceIdType.MESH
F32 = jnp.float32
PIX = 512
ROUNDS = 4
SUBS = 128
N_SUB = 32
N_SURF = 4
WIN = 136
PART = 40
BAND = 3


def spline_np(t):
    first = t**3 / 6.0
    second = (-3.0 * t**3 + 12.0 * t**2 - 12.0 * t + 4.0) / 6.0
    third = (3.0 * t**3 - 24.0 * t**2 + 60.0 * t - 44.0) / 6.0
    fourth = (4.0 - t) ** 3 / 6.0
    inner = np.where(t < 1, first, np.where(t < 2, second, np.where(t < 3, third, fourth)))
    return np.where((t < 0) | (t >= 4), 0.0, inner)


def table_np(rows, cols):
    return spline_np(np.arange(rows)[:, None] * 0.25 - np.arange(cols)[None, :] + 3.0)


COL_TABLE = np.rint(384 * table_np(PIX, 256)).astype(np.float32).astype(ml_dtypes.bfloat16)
ROW_TABLE_T = np.rint(384 * table_np(128, PART)).T.astype(np.float32).astype(ml_dtypes.bfloat16)

_FULL = table_np(PIX, 256)
_U = (np.arange(PIX) - 255.5) / 256.0
COL_NORMAL = (_FULL.T @ _FULL).astype(np.float32)
_NORMAL = _FULL.T @ _FULL
COL_SUMS = np.stack(
    [_FULL.T @ np.ones(PIX), _FULL.T @ _U, _FULL.T @ _U**2, np.diag(_NORMAL)]
).astype(np.float32)
COL_SUMS = np.concatenate([COL_SUMS, np.zeros((4, 256), np.float32)])
N_COEF = 131
_QUANT = np.zeros((N_COEF, 10))
for _a in range(N_COEF):
    for _d in range(-BAND, BAND + 1):
        if 0 <= _a + _d < N_COEF:
            _QUANT[_a, _d + BAND] = _NORMAL[_a, _a + _d]
_QUANT[:, 7:] = np.stack([_FULL.T @ np.ones(PIX), _FULL.T @ _U, _FULL.T @ _U**2], 1)[:N_COEF]
EDGES = (0, 1, 2, 128, 129, 130)
_ROW_U2 = [float((_U**k).sum()) for k in range(5)]
_MID = _QUANT[64]
_VAR = float(_MID[9] - 4.0 * ((4.0 * 63 - 255.5) / 256.0) ** 2)


def exact_dot(table, value):
    high = value.astype(jnp.bfloat16)
    low = (value - high.astype(F32)).astype(jnp.bfloat16)
    return jnp.dot(table, high, preferred_element_type=F32) + jnp.dot(
        table, low, preferred_element_type=F32
    )


def exact_dot_right(value, table):
    high = value.astype(jnp.bfloat16)
    low = (value - high.astype(F32)).astype(jnp.bfloat16)
    return jnp.dot(high, table, preferred_element_type=F32) + jnp.dot(
        low, table, preferred_element_type=F32
    )


STAGES = 5


def hop(s, kind):
    if kind == 0:
        return s + 1 - 2 * (s % 2)
    if kind == 1:
        return s + 3 - 2 * (s % 4)
    if kind == 2:
        return s + 4 - 8 * ((s // 4) % 2)
    if kind == 3:
        return s + 8 - 16 * ((s // 8) % 2)
    return s + 24 - 16 * (s // 8)


def taken(mask, kind):
    bit = [(mask >> n) & 1 for n in range(5)]
    return (bit[0] + bit[1]) % 2 if kind == 0 else (
        (bit[3] + bit[4]) % 2 if kind == 3 else bit[{1: 1, 2: 2, 4: 4}[kind]]
    )


def setup_kernel(masks, offsets, sections, starts, blocks, info_ref, turns, place_ref):
    s, t = lax.axis_index("sub"), lax.axis_index("surf")

    def put(row, value):
        info_ref[row : row + 1] = jnp.full((1, PIX), value, jnp.int32)

    for r in range(ROUNDS):
        other = jnp.bitwise_xor(s, masks[r])
        lower = s < other
        put(r, jnp.where(lower, 1, 0))
        pair = 4 * jnp.minimum(s, other)
        for k in range(STAGES):
            put(4 + 4 * k + r, taken(masks[r], (k + r) % 5))
        for j in range(4):
            shift = offsets[r, pair + j]
            put(24 + 4 * j + r, shift)
            turns[4 * r + j] = jnp.where(lower, shift, (640 - shift) % 512)
    lanes = lax.broadcasted_iota(jnp.int32, (1, 128), 1)
    place = jnp.zeros((1, 128), jnp.int32)
    start = [jnp.int32(0), jnp.int32(0)]
    block = [jnp.int32(0), jnp.int32(0)]
    first = jnp.where(t == 0, 1, 0)
    for j in range(4):
        slot = jnp.int32(0)
        for i in range(j):
            slot = slot + jnp.where(sections[i, 0] == sections[j, 0], 1, 0)
        put(40 + j, 2 * sections[j, 0] + slot)
        for c in range(2):
            here = jnp.where((sections[j, 0] == t) & (slot == c), 1, 0)
            start[c] = start[c] + here * starts[j]
            block[c] = block[c] + here * blocks[j]
        for q, value in enumerate((sections[j, 0], starts[j], blocks[j])):
            place = jnp.where(lanes == 64 + 8 * j + q, first * value, place)
    for c in range(2):
        put(44 + c, start[c])
        put(46 + c, block[c])
    place_ref[...] = place.astype(F32)


def setup(masks, offsets, sections, starts, blocks):
    smem = pl.BlockSpec(memory_space=pltpu.SMEM)
    vmem = pl.BlockSpec(memory_space=pltpu.VMEM)
    return pl.pallas_call(
        setup_kernel,
        out_shape=(
            jax.ShapeDtypeStruct((48, PIX), jnp.int32),
            jax.ShapeDtypeStruct((16,), jnp.int32),
            jax.ShapeDtypeStruct((1, 128), F32),
        ),
        in_specs=[smem] * 5,
        out_specs=(vmem, smem, vmem),
        name="setup",
    )(masks, offsets, sections, starts, blocks)


def main_kernel(
    turns,
    info_ref,
    h_ref,
    place_ref,
    surf_ref,
    ct_ref,
    rt_ref,
    shared_ref,
    back_ref,
    halo_ref,
    pay,
    recv,
    proj,
    send,
    parts,
    win,
    metas,
    part,
    slots,
    rows_in,
    total,
    sems,
    part_sems,
    meta_sems,
    win_sems,
    sum_sems,
    halo_sems,
    near_sems,
    far_sems,
    own_sems,
):
    s, t = lax.axis_index("sub"), lax.axis_index("surf")
    x = s % 4
    base = s - x
    b = s // 4
    ring = ((s + 1) % N_SUB, (s + N_SUB - 1) % N_SUB)
    barrier = pltpu.get_barrier_semaphore()

    def greet(sub, surf):
        pl.semaphore_signal(barrier, inc=1, device_id={"sub": sub, "surf": surf}, device_id_type=MESH)

    for k in range(1, 4):
        greet(s, (t + k) % 4)
        greet(base + (x + k) % 4, t)
    for k in range(1, 8):
        greet(((b + k) % 8) * 4 + x, t)
    for to in ring:
        greet(to, t)

    def flag(row, width):
        return info_ref[row : row + 1, 0:width] == 1

    def first(j, carry):
        for r in range(ROUNDS):
            pay[0, r, j] = jnp.where(flag(r, 384), h_ref[j, 64:128, 128:512], h_ref[j, 0:64, 0:384])
        return carry

    lax.fori_loop(0, 4, first, 0)
    pl.semaphore_wait(barrier, 15)

    def remote(src, dst, pair, at, sub, surf):
        return pltpu.make_async_remote_copy(
            src_ref=src,
            dst_ref=dst,
            send_sem=pair.at[(0,) + at],
            recv_sem=pair.at[(1,) + at],
            device_id={"sub": sub, "surf": surf},
            device_id_type=MESH,
        )

    def copy_of(k, r, j):
        return remote(pay.at[k, r, j], recv.at[k, r, j], sems, (k, r, j), hop(s, (k + r) % 5), t)

    def begin(j, carry):
        for r in range(ROUNDS):
            copy_of(0, r, j).start()
        return carry

    lax.fori_loop(0, 4, begin, 0)

    def forward(k):
        def one(j, carry):
            for r in range(ROUNDS):
                copy_of(k, r, j).wait_recv()
                pay[k + 1, r, j] = jnp.where(
                    flag(4 + 4 * k + r, 384), recv[k, r, j], pay[k, r, j]
                )
            for r in range(ROUNDS):
                copy_of(k + 1, r, j).start()
            return carry

        lax.fori_loop(0, 4, one, 0)

    halos = [
        remote(surf_ref.at[pl.ds(24 - 24 * n, 8), :], halo_ref.at[n], halo_sems, (n,), ring[n], t)
        for n in range(2)
    ]
    for copy in halos:
        copy.start()

    def flatten(j, carry):
        wide = exact_dot_right(h_ref[j], ct_ref[...])
        proj[j] = exact_dot(rt_ref[...], wide) * (1.0 / (384.0 * 384.0))
        return carry

    lax.fori_loop(0, 4, flatten, 0)
    for section in range(4):
        tails = []
        for c in range(2):
            body = jnp.zeros((PART, 128), F32)
            tail = jnp.zeros((PART, 128), F32)
            for j in range(4):
                chosen = info_ref[40 + j : 41 + j, 0:128] == 2 * section + c
                body = body + jnp.where(chosen, proj[j, :, 0:128], 0.0)
                tail = tail + jnp.where(chosen, proj[j, :, 128:256], 0.0)
            send[section, c] = body
            tails.append(tail)
        send[section, 2] = tails[0] + pltpu.roll(tails[1], 64, 1)
    own_part = pltpu.make_async_copy(send.at[t], parts.at[t], own_sems.at[0])
    own_meta = pltpu.make_async_copy(
        info_ref.at[pl.ds(40, 8), pl.ds(0, 256)], metas.at[x], own_sems.at[1]
    )
    own_part.start()
    own_meta.start()
    part_copies = [
        remote(send.at[(t + k) % 4], parts.at[t], part_sems, (k,), s, (t + k) % 4)
        for k in range(1, 4)
    ]
    meta_copies = [
        remote(
            info_ref.at[pl.ds(40, 8), pl.ds(0, 256)],
            metas.at[x],
            meta_sems,
            (k,),
            base + (x + k) % 4,
            t,
        )
        for k in range(1, 4)
    ]
    for copy in part_copies + meta_copies:
        copy.start()
    forward(0)
    own_part.wait()
    own_meta.wait()
    for copy in part_copies:
        copy.wait()
    for e in range(3):
        win[x, e] = jnp.zeros((WIN, 128), F32)
        for p in range(4):
            rows = pl.ds(32 * p, PART)
            win[x, e, rows, :] = win[x, e, rows, :] + parts[p, e]
    win_copies = [
        remote(win.at[x], win.at[x], win_sems, (k,), base + (x + k) % 4, t) for k in range(1, 4)
    ]
    for copy in win_copies:
        copy.start()
    forward(1)
    for copy in meta_copies + win_copies:
        copy.wait()
    local = lax.broadcasted_iota(jnp.int32, (256, WIN), 0)
    wanted = (local // 32) * 128 + 32 * x + local % 32 - lax.broadcasted_iota(jnp.int32, (256, WIN), 1)
    narrow = lax.broadcasted_iota(jnp.int32, (WIN, 128), 1) < 64
    part[...] = jnp.zeros_like(part)

    def spread(q, carry):
        added = jnp.zeros((256, PIX), F32)
        for c in range(2):
            pick = jnp.where(wanted == metas[q, 4 + c : 5 + c, 0:WIN], 1.0, 0.0).astype(jnp.bfloat16)
            block = metas[q, 6 + c : 7 + c, 0:128]
            tail = win[q, 2] if c == 0 else pltpu.roll(win[q, 2], 64, 1)
            tail = jnp.where(narrow, tail, 0.0)
            columns = [
                jnp.where(block == n, win[q, c], 0.0) + jnp.where(block == n - 1, tail, 0.0)
                for n in range(4)
            ]
            added = added + exact_dot(pick, jnp.concatenate(columns, axis=1))
        part[...] = part[...] + added.reshape(8, 32, PIX)
        return carry

    lax.fori_loop(0, 4, spread, 0)
    sum_copies = [
        remote(part.at[(b + k) % 8], slots.at[k], sum_sems, (k,), ((b + k) % 8) * 4 + x, t)
        for k in range(1, 8)
    ]
    for copy in sum_copies:
        copy.start()
    forward(2)
    forward(3)

    xs = lax.broadcasted_iota(jnp.int32, (1, PIX), 1)
    ux = (xs.astype(F32) - 255.5) * (1.0 / 256.0)
    lanes = lax.broadcasted_iota(jnp.int32, (1, 128), 1)
    k = STAGES - 1

    def last(j, row):
        for r in range(ROUNDS):
            lower = flag(r, PIX)
            ys = lax.broadcasted_iota(jnp.int32, (64, 1), 0) + (128 * t + 64)
            uy = ((ys - 64 * info_ref[r : r + 1, 0:1]).astype(F32) - 255.5) * (1.0 / 256.0)
            copy_of(k, r, j).wait_recv()
            came = jnp.where(flag(4 + 4 * k + r, 384), recv[k, r, j], pay[k, r, j])
            shift = info_ref[pl.ds(24 + 4 * j + r, 1), :]
            padded = jnp.concatenate([came, jnp.zeros((64, 128), F32)], axis=1)
            moved = pltpu.roll(padded, turns[4 * r + j], 1)
            inside = jnp.where(lower, xs - shift, PIX - 1 - shift - xs) >= 0
            own = jnp.where(lower, h_ref[j, 0:64], h_ref[j, 64:128])
            value = jnp.where(inside, jnp.tanh(0.5 * (own - moved)), 0.0)
            value_y = value * uy
            sum0 = jnp.sum(value, axis=0, keepdims=True)
            sum1 = jnp.sum(value_y, axis=0, keepdims=True)
            sum2 = jnp.sum(value_y * uy, axis=0, keepdims=True)
            rows = (sum0, ux * sum0, sum1, ux * ux * sum0 + sum2)
            for q in range(4):
                row = jnp.where(
                    lanes == 16 * j + 4 * r + q, jnp.sum(rows[q], axis=1, keepdims=True), row
                )
        return row

    total[0] = lax.fori_loop(0, 4, last, place_ref[...])
    near = [
        remote(total.at[0], rows_in.at[n], near_sems, (n,), s, (t + n) % 4) for n in range(1, 4)
    ]
    for copy in near:
        copy.start()

    def settle(j, carry):
        for k in range(STAGES):
            for r in range(ROUNDS):
                copy_of(k, r, j).wait_send()
        return carry

    lax.fori_loop(0, 4, settle, 0)
    for copy in near:
        copy.wait()
    total[1] = (total[0] + rows_in[1]) + (rows_in[2] + rows_in[3])
    own = pltpu.make_async_copy(total.at[1], shared_ref.at[s], own_sems.at[2])
    own.start()

    def far(n):
        return remote(total.at[1], shared_ref.at[s], far_sems, (n,), (s + n) % N_SUB, t)

    lax.fori_loop(1, N_SUB, lambda n, c: (far(n).start(), c)[1], 0)
    for copy in sum_copies + halos:
        copy.wait()
    summed = part[b]
    for n in range(1, 8):
        summed = summed + slots[n]
    back_ref[...] = summed
    own.wait()
    lax.fori_loop(1, N_SUB, lambda n, c: (far(n).wait(), c)[1], 0)


def main(turns, info, heights, places, surface):
    smem = pl.BlockSpec(memory_space=pltpu.SMEM)
    vmem = pl.BlockSpec(memory_space=pltpu.VMEM)
    dma = pltpu.SemaphoreType.DMA
    return pl.pallas_call(
        main_kernel,
        out_shape=(
            jax.ShapeDtypeStruct((N_SUB, 1, 128), F32),
            jax.ShapeDtypeStruct((32, PIX), F32),
            jax.ShapeDtypeStruct((2, 8, PIX), F32),
        ),
        in_specs=[smem] + [vmem] * 6,
        out_specs=(vmem, vmem, vmem),
        scratch_shapes=[
            pltpu.VMEM((STAGES, ROUNDS, 4, 64, 384), F32),
            pltpu.VMEM((STAGES, ROUNDS, 4, 64, 384), F32),
            pltpu.VMEM((4, PART, 256), F32),
            pltpu.VMEM((4, 3, PART, 128), F32),
            pltpu.VMEM((4, 3, PART, 128), F32),
            pltpu.VMEM((4, 3, WIN, 128), F32),
            pltpu.VMEM((4, 8, 256), jnp.int32),
            pltpu.VMEM((8, 32, PIX), F32),
            pltpu.VMEM((8, 32, PIX), F32),
            pltpu.VMEM((4, 1, 128), F32),
            pltpu.VMEM((2, 1, 128), F32),
            dma((2, STAGES, ROUNDS, 4)),
            dma((2, 4)),
            dma((2, 4)),
            dma((2, 4)),
            dma((2, 8)),
            dma((2, 2)),
            dma((2, 4)),
            dma((2, N_SUB)),
            dma((3,)),
        ],
        compiler_params=pltpu.CompilerParams(collective_id=0, has_side_effects=True),
        name="main",
    )(turns, info, heights, places, surface, jnp.asarray(COL_TABLE), jnp.asarray(ROW_TABLE_T))


def swap_lanes(value, width, bit, lanes):
    swapped = jnp.where(
        (lanes & width) != 0,
        pltpu.roll(value, width, 1),
        pltpu.roll(value, 128 - width, 1),
    )
    return jnp.where(bit == 1, swapped, value)


def finish_kernel(masks, off_ref, m_ref, s_ref, back_ref, halo_ref, gc_ref, cs_ref, par_ref, out_ref):
    me, section = lax.axis_index("sub"), lax.axis_index("surf")
    lane1 = lax.broadcasted_iota(jnp.int32, (1, 128), 1)
    sub1 = lane1 // 4
    rows16 = lax.broadcasted_iota(jnp.int32, (16, 128), 0)
    lane16 = lax.broadcasted_iota(jnp.int32, (16, 128), 1)
    mask16 = jnp.zeros((16, 128), jnp.int32)
    for r in range(ROUNDS):
        mask16 = jnp.where(rows16 // 4 == r, masks[r], mask16)
    spread = (
        lax.broadcasted_iota(jnp.int32, (N_SUB, 128), 1) // 4
        == lax.broadcasted_iota(jnp.int32, (N_SUB, 128), 0)
    ).astype(F32)
    table = lax.dot_general(
        m_ref[:, 0, :], spread, (((0,), (0,)), ((), ())), precision=HIGH, preferred_element_type=F32
    )
    own = jnp.zeros((16, 128), F32)
    place = jnp.zeros((8, 128), F32)
    for j in range(4):
        own = jnp.where(lane16 % 4 == j, table[16 * j : 16 * j + 16], own)
        place = jnp.where(lane16[:8] % 4 == j, table[64 + 8 * j : 72 + 8 * j], place)
    other = own
    shifts = off_ref[...]
    mask4 = jnp.concatenate([mask16[4 * r : 4 * r + 1] for r in range(ROUNDS)], axis=0)
    lane4 = lane16[:4]
    other_shift = shifts
    for bit in range(5):
        other = swap_lanes(other, 4 << bit, (mask16 >> bit) & 1, lane16)
        other_shift = swap_lanes(other_shift, 4 << bit, (mask4 >> bit) & 1, lane4)
    lower4 = (lane4 // 4) < jnp.bitwise_xor(lane4 // 4, mask4)
    shifts = jnp.where(lower4, shifts, other_shift)
    delta = jnp.where(lower4, shifts, -shifts).astype(F32) * (1.0 / 256.0)
    rhs = [jnp.zeros((1, 128), F32) for _ in range(4)]
    for r in range(ROUNDS):
        o = [own[4 * r + k : 4 * r + k + 1] for k in range(4)]
        p = [other[4 * r + k : 4 * r + k + 1] for k in range(4)]
        d = delta[r : r + 1]
        rhs[0] = rhs[0] + (o[0] - p[0])
        rhs[1] = rhs[1] + (o[1] - (p[1] + d * p[0]))
        rhs[2] = rhs[2] + (o[2] - p[2])
        rhs[3] = rhs[3] + (o[3] - (p[3] + d * (2.0 * p[1] + d * p[0])))
    column = lax.broadcasted_iota(jnp.int32, (PIX, 128), 0)
    count = jnp.zeros((PIX, 128), F32)
    for r in range(ROUNDS):
        shift = shifts[r : r + 1]
        low = jnp.where(lower4[r : r + 1], shift, 0)
        high = jnp.where(lower4[r : r + 1], PIX, PIX - shift)
        count = count + jnp.where((column >= low) & (column < high), 1.0, 0.0)
    ux = (lax.broadcasted_iota(jnp.int32, (PIX, 1), 0).astype(F32) - 255.5) * (1.0 / 256.0)
    power = []
    term = count
    for k in range(5):
        power.append(jnp.sum(term, axis=0, keepdims=True))
        if k < 4:
            term = term * ux
    y0, y2, y4 = _ROW_U2[0], _ROW_U2[2], _ROW_U2[4]
    g00 = power[0] * y0
    g01 = power[1] * y0
    g03 = power[2] * y0 + power[0] * y2
    g11 = power[2] * y0
    g13 = power[3] * y0 + power[1] * y2
    g22 = power[0] * y2
    g33 = power[4] * y0 + 2.0 * power[2] * y2 + power[0] * y4
    l00 = jnp.sqrt(g00)
    l10 = g01 / l00
    l30 = g03 / l00
    l11 = jnp.sqrt(g11 - l10 * l10)
    l31 = (g13 - l30 * l10) / l11
    l33 = jnp.sqrt(g33 - l30 * l30 - l31 * l31)
    z0 = rhs[0] / l00
    z1 = (rhs[1] - l10 * z0) / l11
    z3 = (rhs[3] - l30 * z0 - l31 * z1) / l33
    p3 = z3 / l33
    p1 = (z1 - l31 * p3) / l11
    p0 = (z0 - l10 * p1 - l30 * p3) / l00
    p2 = rhs[2] / g22
    params = jnp.concatenate([p0, p1, p2, p3], axis=0)
    par_ref[...] = pltpu.roll(params, (128 - 4 * me) % 128, 1)[:, 0:4]
    start = place[1:2].astype(jnp.int32)
    a = lax.broadcasted_iota(jnp.int32, (32, 128), 0) + 32 * me - start
    in_window = (a >= 0) & (a < N_COEF)
    middle = (a > EDGES[2]) & (a < EDGES[3])
    edges = [(a == e).astype(F32) for e in EDGES]

    def quantity(q, inner):
        value = jnp.where(middle, inner, 0.0)
        for e, at in zip(EDGES, edges):
            if _QUANT[e, q] != 0.0:
                value = value + at * float(_QUANT[e, q])
        return value

    centre = (4.0 * (a.astype(F32) - 1.0) - 255.5) * (1.0 / 256.0)
    bands = [quantity(q, float(_MID[q])) for q in range(7)]
    sum0 = quantity(7, 4.0)
    sum1 = quantity(8, 4.0 * centre)
    sum2 = quantity(9, 4.0 * centre * centre + _VAR)
    plane0 = p0 * sum0 + p2 * sum1 + p3 * sum2
    plane1 = p1 * sum0
    plane2 = p3 * sum0
    out_ref[...] = back_ref[...]
    weight = [jnp.zeros((32, 128), F32) for _ in range(4)]
    for c in range(3):
        chosen = (place[0:1] == section.astype(F32)) & (place[2:3] == float(c))
        chosen = chosen.astype(F32)
        band = [jnp.sum(v * chosen, axis=1, keepdims=True) for v in bands]
        plane = [jnp.sum(v * chosen, axis=1, keepdims=True) for v in (plane0, plane1, plane2)]
        cols = pl.ds(128 * c, 256)
        tall = jnp.concatenate([halo_ref[0, :, cols], s_ref[:, cols], halo_ref[1, :, cols]], axis=0)
        normal = jnp.dot(tall, gc_ref[...], precision=HIGH, preferred_element_type=F32)
        taken = plane[0] * cs_ref[0:1] + plane[1] * cs_ref[1:2] + plane[2] * cs_ref[2:3]
        for d in range(-BAND, BAND + 1):
            taken = taken + band[d + BAND] * normal[8 + d : 40 + d]
        out_ref[:, cols] = out_ref[:, cols] - taken
        diag = band[BAND] * cs_ref[3:4]
        weight[c] = weight[c] + diag[:, :128]
        weight[c + 1] = weight[c + 1] + diag[:, 128:]
    for c in range(4):
        cols = pl.ds(128 * c, 128)
        out_ref[:, cols] = s_ref[:, cols] + out_ref[:, cols] / (weight[c] + 1.0)


def finish(masks, offsets, shared, surface, back, halo):
    vmem = pl.BlockSpec(memory_space=pltpu.VMEM)
    return pl.pallas_call(
        finish_kernel,
        out_shape=(jax.ShapeDtypeStruct((4, 4), F32), jax.ShapeDtypeStruct((32, 512), F32)),
        in_specs=[pl.BlockSpec(memory_space=pltpu.SMEM)] + [vmem] * 7,
        out_specs=(vmem, vmem),
        name="finish",
    )(masks, offsets, shared, surface, back, halo, jnp.asarray(COL_NORMAL), jnp.asarray(COL_SUMS))


def per_device(heights, masks, offsets, sections, row_starts, col_blocks, surface):
    info, turns, places = setup(masks, offsets, sections, row_starts, col_blocks)
    shared, back, halo = main(turns, info, heights, places, surface)
    params, fitted = finish(masks, offsets, shared, surface, back, halo)
    return params, fitted


def solution(mesh):
    in_specs = (
        P("sub", "surf", None),
        P(),
        P(),
        P("sub", None),
        P("sub"),
        P("sub"),
        P("sub", "surf"),
    )
    out_specs = (P(None, "sub"), P("sub", "surf"))
    return jax.shard_map(
        per_device, mesh=mesh, in_specs=in_specs, out_specs=out_specs, check_vma=False
    )
```

time: 133 us -> 81.2 us (0.61)
  Pallas kernels: 107 us -> 79 us
  between operations: 13.4 us -> 0.65 us
  other arithmetic: 6.95 us -> 0 us
  local copies, waits for them, and re-layouts: 5.48 us -> 1.31 us
    pallas_call x5 -> x2, Pallas kernels: 104 us -> 76.1 us  [the longest x1 74.6 us: main(): pl.pallas_call(main_kernel, out_shape=(jax.ShapeDtypeStruct((N_SUB, 1, 12...]
    concatenate x2 -> x0, other arithmetic: 1.85 us -> none  [the longest x1 1.26 us: per_device(): jnp.concatenate([jnp.stack([me_sub, me_surf]), masks]).astype(jnp.int32)]
    reduce_sum x2 -> x0, other arithmetic: 1.79 us -> none  [the longest x1 0.91 us: per_device(): slot_of = jnp.sum(earlier.astype(jnp.int32), axis=1)]
    gather x3 -> x0, local copies, waits for them, and re-layouts: 1.54 us -> none  [per_device(): shift = jnp.take_along_axis(offsets, pair, axis=1)]
    broadcast_in_dim x5 -> x0, local copies, waits for them, and re-layouts: 1.52 us -> none  [the longest x1 0.7 us: per_device(): steps = jnp.broadcast_to(steps[:, None], (40, PIX))]
    slice x2 -> x0, local copies, waits for them, and re-layouts: 1.5 us -> none  [the longest x1 0.84 us: per_device(): metas[:, 0, 0:2].reshape(8)]
where the time goes in v3:
time: 81.2 us; the launch traced here: 81 us
  Pallas kernels  79 us (97%)
  local copies, waits for them, and re-layouts  1.31 us (2%)
    pallas_call x1, Pallas kernels, main(): pl.pallas_call(main_kernel, out_shape=(jax.ShapeDtypeStruct((N_SUB, 1, 12...  74.6 us
    pallas_call x1, Pallas kernels, finish(): pl.pallas_call(finish_kernel, out_shape=(jax.ShapeDtypeStruct((4, 4), F32...  2.88 us

profile of v3, /device:TPU:0, one launch (start us, length us, event | category | flops | bytes accessed | tf_op | source)
XLA Modules:
  0.0 81.0 jit_solution(11435569717960844335)
XLA Ops:
  0.6 1.3 %copy.13.sections = s32[4,1]{1,0:T(4,128)} copy(s32[4,1]{0,1:T(1,128)} %param.14) | data formatting | bytes 32 | tf_op args[3]
  1.9 1.5 %setup.1 = (s32[48,512]{1,0:T(8,128)}, s32[16]{0:T(128)}, f32[1,128]{1,0:T(1,128)}) custom-call(s32[4]{0:T(128)} %masks.3, s32[4,128]{1,0:T(4,128)} %off_ref.1, s32[4,1]{1,0:T(4,128)} %copy.13.sections, s32[4]{0:T(128)} %starts.1, s32[4]{0:T(128)} %blocks.1), custom_call_target="tpu_custom_call" | custom-call | tf_op jit(solution)/shard_map/setup/pallas_call | solution.py:140
  3.5 74.6 %main.1 = (f32[32,1,128]{2,1,0:T(1,128)}, f32[32,512]{1,0:T(8,128)}, f32[2,8,512]{2,1,0:T(8,128)}) custom-call(s32[16]{0:T(128)} %get-tuple-element.8.turns, s32[48,512]{1,0:T(8,128)} %get-tuple-element.9.info_ref, f32[4,128,512]{2,1,0:T(8,128)} %h_ref.1, f32[1,128]{1,0:T(1,128)} %get-tuple-element.10.place_ref, f32[32,512]{1,0:T(8,128)} %s_ref.1, ...), custom_call_target="tpu_custom_call" | custom-call | tf_op jit(solution)/shard_map/main/pallas_call | solution.py:410
  78.1 2.9 %finish.1 = (f32[4,4]{1,0:T(4,128)}, f32[32,512]{1,0:T(8,128)}) custom-call(s32[4]{0:T(128)} %masks.3, s32[4,128]{1,0:T(4,128)} %off_ref.1, f32[32,1,128]{2,1,0:T(1,128)} %get-tuple-element.11.m_ref, f32[32,512]{1,0:T(8,128)} %s_ref.1, f32[32,512]{1,0:T(8,128)} %get-tuple-element.12.back_ref, f32[2,8,512]{2,1,0:T(8,128)} %get-tuple-element.13.halo_ref, ...), custom_call_target="tpu_custom_call" | custom-call | tf_op jit(solution)/shard_map/finish/pallas_call | solution.py:578

commit v4 on v3

--- a/solution.py
+++ b/solution.py
@@ -1,3 +1,5 @@
+import functools
+
 import jax
 import jax.numpy as jnp
 import ml_dtypes
@@ -74,6 +76,7 @@
 
 
 STAGES = 5
+STREAMS = ((0, 24), (24, 24), (48, 24), (72, 24), (96, 32), (128, 24), (152, 24), (176, 24), (200, 24), (224, 32))
 
 
 def hop(s, kind):
@@ -95,7 +98,7 @@
     )
 
 
-def setup_kernel(masks, offsets, sections, starts, blocks, info_ref, turns, place_ref):
+def setup_kernel(masks, offsets, sections, starts, blocks, info_ref, turns, place_ref, fits_ref):
     s, t = lax.axis_index("sub"), lax.axis_index("surf")
 
     def put(row, value):
@@ -106,12 +109,21 @@
         lower = s < other
         put(r, jnp.where(lower, 1, 0))
         pair = 4 * jnp.minimum(s, other)
-        for k in range(STAGES):
-            put(4 + 4 * k + r, taken(masks[r], (k + r) % 5))
+        for kind in range(STAGES):
+            put(4 + 4 * kind + r, taken(masks[r], kind))
         for j in range(4):
             shift = offsets[r, pair + j]
             put(24 + 4 * j + r, shift)
             turns[4 * r + j] = jnp.where(lower, shift, (640 - shift) % 512)
+    fits = jnp.int32(1)
+    for kind in range(STAGES):
+        need = [taken(masks[r], kind) for r in range(ROUNDS)]
+        rest = need[3]
+        for n in range(3):
+            put(48 + 3 * kind + n, rest * (1 - need[n]))
+            rest = rest * need[n]
+        fits = fits * (1 - rest)
+    fits_ref[0] = fits
     lanes = lax.broadcasted_iota(jnp.int32, (1, 128), 1)
     place = jnp.zeros((1, 128), jnp.int32)
     start = [jnp.int32(0), jnp.int32(0)]
@@ -120,13 +132,13 @@
     for j in range(4):
         slot = jnp.int32(0)
         for i in range(j):
-            slot = slot + jnp.where(sections[i, 0] == sections[j, 0], 1, 0)
-        put(40 + j, 2 * sections[j, 0] + slot)
+            slot = slot + jnp.where(sections[i] == sections[j], 1, 0)
+        put(40 + j, 2 * sections[j] + slot)
         for c in range(2):
-            here = jnp.where((sections[j, 0] == t) & (slot == c), 1, 0)
+            here = jnp.where((sections[j] == t) & (slot == c), 1, 0)
             start[c] = start[c] + here * starts[j]
             block[c] = block[c] + here * blocks[j]
-        for q, value in enumerate((sections[j, 0], starts[j], blocks[j])):
+        for q, value in enumerate((sections[j], starts[j], blocks[j])):
             place = jnp.where(lanes == 64 + 8 * j + q, first * value, place)
     for c in range(2):
         put(44 + c, start[c])
@@ -140,17 +152,19 @@
     return pl.pallas_call(
         setup_kernel,
         out_shape=(
-            jax.ShapeDtypeStruct((48, PIX), jnp.int32),
+            jax.ShapeDtypeStruct((64, PIX), jnp.int32),
             jax.ShapeDtypeStruct((16,), jnp.int32),
             jax.ShapeDtypeStruct((1, 128), F32),
+            jax.ShapeDtypeStruct((1,), jnp.int32),
         ),
         in_specs=[smem] * 5,
-        out_specs=(vmem, smem, vmem),
+        out_specs=(vmem, smem, vmem, smem),
         name="setup",
     )(masks, offsets, sections, starts, blocks)
 
 
 def main_kernel(
+    count,
     turns,
     info_ref,
     h_ref,
@@ -162,6 +176,7 @@
     back_ref,
     halo_ref,
     pay,
+    outs,
     recv,
     proj,
     send,
@@ -203,12 +218,23 @@
     def flag(row, width):
         return info_ref[row : row + 1, 0:width] == 1
 
-    def first(j, carry):
-        for r in range(ROUNDS):
-            pay[0, r, j] = jnp.where(flag(r, 384), h_ref[j, 64:128, 128:512], h_ref[j, 0:64, 0:384])
-        return carry
-
-    lax.fori_loop(0, 4, first, 0)
+    for r in range(ROUNDS):
+        for j in range(4):
+            pay[r, 64 * j : 64 * j + 64] = jnp.where(
+                flag(r, 384), h_ref[j, 64:128, 128:512], h_ref[j, 0:64, 0:384]
+            )
+
+    def load(k, q):
+        first, size = STREAMS[q]
+        rows = pl.ds(first, size)
+        for n in range(count):
+            value = pay[n, rows, :]
+            if count < ROUNDS:
+                value = jnp.where(flag(48 + 3 * ((k + q) % 5) + n, 384), pay[3, rows, :], value)
+            outs[k, pl.ds(count * first + n * size, size), :] = value
+
+    for q in range(10):
+        load(0, q)
     pl.semaphore_wait(barrier, 15)
 
     def remote(src, dst, pair, at, sub, surf):
@@ -221,28 +247,35 @@
             device_id_type=MESH,
         )
 
-    def copy_of(k, r, j):
-        return remote(pay.at[k, r, j], recv.at[k, r, j], sems, (k, r, j), hop(s, (k + r) % 5), t)
-
-    def begin(j, carry):
-        for r in range(ROUNDS):
-            copy_of(0, r, j).start()
-        return carry
-
-    lax.fori_loop(0, 4, begin, 0)
+    def copy_of(k, q):
+        first, size = STREAMS[q]
+        rows = pl.ds(count * first, count * size)
+        return remote(
+            outs.at[k, rows, :], recv.at[k, rows, :], sems, (k, q), hop(s, (k + q) % 5), t
+        )
+
+    for q in range(10):
+        copy_of(0, q).start()
+
+    def take(k, q):
+        first, size = STREAMS[q]
+        rows = pl.ds(first, size)
+        kind = (k + q) % 5
+        copy_of(k, q).wait_recv()
+        came = [recv[k, pl.ds(count * first + n * size, size), :] for n in range(count)]
+        for n in range(count):
+            pay[n, rows, :] = jnp.where(flag(4 + 4 * kind + n, 384), came[n], pay[n, rows, :])
+        if count < ROUNDS:
+            extra = pay[3, rows, :]
+            for n in range(count):
+                extra = jnp.where(flag(48 + 3 * kind + n, 384), came[n], extra)
+            pay[3, rows, :] = extra
 
     def forward(k):
-        def one(j, carry):
-            for r in range(ROUNDS):
-                copy_of(k, r, j).wait_recv()
-                pay[k + 1, r, j] = jnp.where(
-                    flag(4 + 4 * k + r, 384), recv[k, r, j], pay[k, r, j]
-                )
-            for r in range(ROUNDS):
-                copy_of(k + 1, r, j).start()
-            return carry
-
-        lax.fori_loop(0, 4, one, 0)
+        for q in sorted(range(10), key=lambda q: (q // 5, (k + q) % 5 == 2)):
+            take(k, q)
+            load(k + 1, q)
+            copy_of(k + 1, q).start()
 
     halos = [
         remote(surf_ref.at[pl.ds(24 - 24 * n, 8), :], halo_ref.at[n], halo_sems, (n,), ring[n], t)
@@ -308,6 +341,7 @@
     for copy in win_copies:
         copy.start()
     forward(1)
+    forward(2)
     for copy in meta_copies + win_copies:
         copy.wait()
     local = lax.broadcasted_iota(jnp.int32, (256, WIN), 0)
@@ -337,23 +371,23 @@
     ]
     for copy in sum_copies:
         copy.start()
-    forward(2)
     forward(3)
 
     xs = lax.broadcasted_iota(jnp.int32, (1, PIX), 1)
     ux = (xs.astype(F32) - 255.5) * (1.0 / 256.0)
     lanes = lax.broadcasted_iota(jnp.int32, (1, 128), 1)
-    k = STAGES - 1
-
-    def last(j, row):
+    row = place_ref[...]
+    done = 0
+    for j in range(4):
+        while done < 10 and STREAMS[done][0] < 64 * j + 64:
+            take(STAGES - 1, done)
+            done += 1
         for r in range(ROUNDS):
             lower = flag(r, PIX)
             ys = lax.broadcasted_iota(jnp.int32, (64, 1), 0) + (128 * t + 64)
             uy = ((ys - 64 * info_ref[r : r + 1, 0:1]).astype(F32) - 255.5) * (1.0 / 256.0)
-            copy_of(k, r, j).wait_recv()
-            came = jnp.where(flag(4 + 4 * k + r, 384), recv[k, r, j], pay[k, r, j])
-            shift = info_ref[pl.ds(24 + 4 * j + r, 1), :]
-            padded = jnp.concatenate([came, jnp.zeros((64, 128), F32)], axis=1)
+            shift = info_ref[24 + 4 * j + r : 25 + 4 * j + r, :]
+            padded = jnp.concatenate([pay[r, 64 * j : 64 * j + 64], jnp.zeros((64, 128), F32)], axis=1)
             moved = pltpu.roll(padded, turns[4 * r + j], 1)
             inside = jnp.where(lower, xs - shift, PIX - 1 - shift - xs) >= 0
             own = jnp.where(lower, h_ref[j, 0:64], h_ref[j, 64:128])
@@ -367,22 +401,16 @@
                 row = jnp.where(
                     lanes == 16 * j + 4 * r + q, jnp.sum(rows[q], axis=1, keepdims=True), row
                 )
-        return row
-
-    total[0] = lax.fori_loop(0, 4, last, place_ref[...])
+    total[0] = row
     near = [
         remote(total.at[0], rows_in.at[n], near_sems, (n,), s, (t + n) % 4) for n in range(1, 4)
     ]
     for copy in near:
         copy.start()
 
-    def settle(j, carry):
-        for k in range(STAGES):
-            for r in range(ROUNDS):
-                copy_of(k, r, j).wait_send()
-        return carry
-
-    lax.fori_loop(0, 4, settle, 0)
+    for k in range(STAGES):
+        for q in range(10):
+            copy_of(k, q).wait_send()
     for copy in near:
         copy.wait()
     total[1] = (total[0] + rows_in[1]) + (rows_in[2] + rows_in[3])
@@ -403,12 +431,12 @@
     lax.fori_loop(1, N_SUB, lambda n, c: (far(n).wait(), c)[1], 0)
 
 
-def main(turns, info, heights, places, surface):
+def main(count, turns, info, heights, places, surface):
     smem = pl.BlockSpec(memory_space=pltpu.SMEM)
     vmem = pl.BlockSpec(memory_space=pltpu.VMEM)
     dma = pltpu.SemaphoreType.DMA
     return pl.pallas_call(
-        main_kernel,
+        functools.partial(main_kernel, count),
         out_shape=(
             jax.ShapeDtypeStruct((N_SUB, 1, 128), F32),
             jax.ShapeDtypeStruct((32, PIX), F32),
@@ -417,8 +445,9 @@
         in_specs=[smem] + [vmem] * 6,
         out_specs=(vmem, vmem, vmem),
         scratch_shapes=[
-            pltpu.VMEM((STAGES, ROUNDS, 4, 64, 384), F32),
-            pltpu.VMEM((STAGES, ROUNDS, 4, 64, 384), F32),
+            pltpu.VMEM((ROUNDS, 256, 384), F32),
+            pltpu.VMEM((STAGES, count * 256, 384), F32),
+            pltpu.VMEM((STAGES, count * 256, 384), F32),
             pltpu.VMEM((4, PART, 256), F32),
             pltpu.VMEM((4, 3, PART, 128), F32),
             pltpu.VMEM((4, 3, PART, 128), F32),
@@ -428,7 +457,7 @@
             pltpu.VMEM((8, 32, PIX), F32),
             pltpu.VMEM((4, 1, 128), F32),
             pltpu.VMEM((2, 1, 128), F32),
-            dma((2, STAGES, ROUNDS, 4)),
+            dma((2, STAGES, 10)),
             dma((2, 4)),
             dma((2, 4)),
             dma((2, 4)),
@@ -438,7 +467,7 @@
             dma((2, N_SUB)),
             dma((3,)),
         ],
-        compiler_params=pltpu.CompilerParams(collective_id=0, has_side_effects=True),
+        compiler_params=pltpu.CompilerParams(collective_id=count - 3, has_side_effects=True),
         name="main",
     )(turns, info, heights, places, surface, jnp.asarray(COL_TABLE), jnp.asarray(ROW_TABLE_T))
 
@@ -585,8 +614,17 @@
 
 
 def per_device(heights, masks, offsets, sections, row_starts, col_blocks, surface):
-    info, turns, places = setup(masks, offsets, sections, row_starts, col_blocks)
-    shared, back, halo = main(turns, info, heights, places, surface)
+    info, turns, places, fits = setup(masks, offsets, sections.reshape(4), row_starts, col_blocks)
+    shared, back, halo = lax.cond(
+        fits[0] == 1,
+        functools.partial(main, 3),
+        functools.partial(main, 4),
+        turns,
+        info,
+        heights,
+        places,
+        surface,
+    )
     params, fitted = finish(masks, offsets, shared, surface, back, halo)
     return params, fitted
 

time: 81.2 us -> 71.8 us (0.88)
  Pallas kernels: 79 us -> 70.3 us
  local copies, waits for them, and re-layouts: 1.31 us -> 0.01 us
    pallas_call x2, Pallas kernels: 76.1 us -> 67.4 us  [the longest x1 65.9 us: main(): pl.pallas_call(functools.partial(main_kernel, count), out_shape=(jax.Shap...]
    unnamed x1 -> x2, local copies, waits for them, and re-layouts: 1.31 us -> 0.01 us
where the time goes in v4:
time: 71.8 us; the launch traced here: 71.6 us
  Pallas kernels  70.3 us (98%)
  between operations  1.31 us (2%)
    pallas_call x1, Pallas kernels, main(): pl.pallas_call(functools.partial(main_kernel, count), out_shape=(jax.Shap...  65.9 us
    pallas_call x1, Pallas kernels, finish(): pl.pallas_call(finish_kernel, out_shape=(jax.ShapeDtypeStruct((4, 4), F32...  2.88 us
    pallas_call x1, Pallas kernels, setup(): pl.pallas_call(setup_kernel, out_shape=(jax.ShapeDtypeStruct((64, PIX), j...  1.49 us

profile of v4, /device:TPU:0, one launch (start us, length us, event | category | flops | bytes accessed | tf_op | source)
XLA Modules:
  0.0 71.6 jit_solution(17628070512535368294)
XLA Ops:
  0.6 0.0 copy-start
  0.6 1.5 %setup.1 = (s32[64,512]{1,0:T(8,128)S(1)}, s32[16]{0:T(128)S(1)}, f32[1,128]{1,0:T(1,128)S(1)}, s32[1]{0:T(128)}) custom-call(s32[4]{0:T(128)} %masks.3, s32[4,128]{1,0:T(4,128)} %off_ref.1, s32[4]{0:T(128)} %bitcast.2, s32[4]{0:T(128)} %starts.1, s32[4]{0:T(128)} %blocks.1), custom_call_target="tpu_custom_call" | custom-call | tf_op jit(solution)/shard_map/setup/pallas_call | solution.py:152
  2.8 0.0 copy-done
  2.8 65.9 %conditional.1 = ((f32[32,1,128]{2,1,0:T(1,128)S(1)}, f32[32,512]{1,0:T(8,128)S(1)}, f32[2,8,512]{2,1,0:T(8,128)S(1)})) conditional(s32[]{:T(128)} %bitcast.1, (s32[16]{0:T(128)S(1)}, s32[64,512]{1,0:T(8,128)S(1)}, f32[4,128,512]{2,1,0:T(8,128)}, f32[1,128]{1,0:T(1,128)S(1)}, f32[32,512]{1,0:T(8,128)}, /*index=5*/bf16[512,256]{1,0:T(8,128)(2,1)}, ...), branch_computations={%region_0.0_spmd, %region_1.0_spmd} | conditional | bytes 8 | solution.py:618
  2.8 65.9 %main.3 = (f32[32,1,128]{2,1,0:T(1,128)S(1)}, f32[32,512]{1,0:T(8,128)S(1)}, f32[2,8,512]{2,1,0:T(8,128)S(1)}) custom-call(s32[16]{0:T(128)S(1)} %get-tuple-element.35.turns, s32[64,512]{1,0:T(8,128)S(1)} %get-tuple-element.36.info_ref, f32[4,128,512]{2,1,0:T(8,128)} %get-tuple-element.37.h_ref, f32[1,128]{1,0:T(1,128)S(1)} %get-tuple-element.38.place_ref, ...), custom_call_target="tpu_custom_call" | custom-call | tf_op jit(solution)/shard_map/cond/branch_1_fun/main/pallas_call | solution.py:438
  68.7 2.9 %finish.1 = (f32[4,4]{1,0:T(4,128)}, f32[32,512]{1,0:T(8,128)}) custom-call(s32[4]{0:T(128)} %masks.3, s32[4,128]{1,0:T(4,128)} %off_ref.1, f32[32,1,128]{2,1,0:T(1,128)S(1)} %get-tuple-element.55.m_ref, f32[32,512]{1,0:T(8,128)} %s_ref.1, f32[32,512]{1,0:T(8,128)S(1)} %get-tuple-element.56.back_ref, f32[2,8,512]{2,1,0:T(8,128)S(1)} %get-tuple-element.57.halo_ref, ...), custom_call_target="tpu_custom_call" | custom-call | tf_op jit(solution)/shard_map/finish/pallas_call | solution.py:607
Async XLA Ops:
  0.6 2.2 %copy-start = (bf16[40,128]{1,0:T(8,128)(2,1)S(1)}, bf16[40,128]{1,0:T(8,128)(2,1)}, u32[]{:S(2)}) copy-start(bf16[40,128]{1,0:T(8,128)(2,1)} %constant.12.clone) | copy-start | bytes 30724
